TPU v7x, 512 devices: a whole 4x8x8 slice. The times are simulated.
512 devices in a mesh: atoms: 128 (over x_hi, z, y), modes: 4 (over x_lo, core).
Axes of the slice: x: 4 (x_hi: 2, x_lo: 2; x = x_hi * 2 + x_lo), y: 8, z: 8, core: 2. Of those that a mesh axis runs over, the one named last changes fastest.
Arguments:
- eigvec: bfloat16 [49152, 2048], P('atoms', 'modes'), may hold values from -6 to 6
- operator_blocks: bfloat16 [384, 8, 128, 128], P('atoms'), may hold values from -0.0008544922 to 0.0008544922
- column_blocks: int32 [384, 8], P('atoms'), may hold values from 0 to 383, as said below
- block_mask: int32 [384, 8], P('atoms'), may hold values 0 or 1
- spectrum: float32 [49152], replicated, may hold values from 0.5 to 20
- mode_index: int32 [2048], replicated, may hold values from 0 to 49151
- linewidth: float32 [2048], replicated, may hold values from 0.05 to 1
Outputs:
- flux_tiles: float32 [2048, 2048], P('modes', 'atoms')
- diffusivity: float32 [2048], P('modes')
Inputs may be any that keep to these rules, and one draw needn't show every extreme that they name: `column_blocks`: the 8 column blocks of row block r are distinct and lie within 4 blocks of r, counted around the cycle of 384 blocks.
All inputs are finite; a program needn't handle non-finite values. No bound on the sum of `block_mask` on one device may be relied on, other than what follows from the above.
Results may differ from a plain program's by a relative error of at most 0.0058.
Values may be sent and summed in bfloat16 or wider, within the bound.
A program may use at most 64 MiB of HBM per device.

v0:
```python
import functools

import jax
import jax.numpy as jnp
from jax import lax
from jax.sharding import Mesh
from jax.sharding import PartitionSpec as P

REACH = 4
ATOMS = ("atoms_0", "atoms_1", "atoms_2")


def with_halo(block, sides, width):
    for axis, dim in sides:
        count = lax.axis_size(axis)
        forward = [(i, i + 1) for i in range(count - 1)]
        forward.append((count - 1, 0))
        backward = [(target, source) for source, target in forward]
        low = lax.ppermute(
            lax.slice_in_dim(block, block.shape[dim] - width, None, axis=dim), axis, forward
        )
        high = lax.ppermute(lax.slice_in_dim(block, 0, width, axis=dim), axis, backward)
        block = jnp.concatenate([low, block, high], axis=dim)
    return block


def from_behind(value, axis, by):
    devices = lax.axis_size(axis)
    return lax.ppermute(value, axis, [(i, (i + by) % devices) for i in range(devices)])


def split_up(value, dim, devices):
    before, after = (value.shape[:dim], value.shape[dim + 1 :])
    return jnp.moveaxis(value.reshape(*before, devices, -1, *after), dim, 0)


def sent_and_summed(value, axis, dim):
    pieces = split_up(value, dim, lax.axis_size(axis))
    arrived = lax.all_to_all(pieces, axis, split_axis=0, concat_axis=0, tiled=True)
    return arrived.astype(jnp.float32).sum(axis=0)


def sum_by_axis(value, axes, dim):
    far, near = axes
    own = sent_and_summed(split_up(value, dim, lax.axis_size(far)), near, dim + 1)
    return jnp.sum(
        lax.all_to_all(own.astype(jnp.bfloat16), far, 0, 0, tiled=True).astype(jnp.float32), axis=0
    )


def over_axes(value, axes):
    return functools.reduce(lax.psum, axes, value)


def pair_weight(row_freq, col_freq, row_width, col_width):
    freq_sum = row_freq[:, None] + col_freq[None, :]
    spacing = row_freq[:, None] - col_freq[None, :]
    mean_width = 0.5 * (row_width[:, None] + col_width[None, :])
    factor = freq_sum * freq_sum / (4.0 * row_freq[:, None] * col_freq[None, :])
    return factor * mean_width / (spacing * spacing + mean_width * mean_width)


def body(eigvec, operator_blocks, column_blocks, block_mask, spectrum, mode_index, linewidth):
    block_width = operator_blocks.shape[2]
    local_blocks = operator_blocks.shape[0]
    own_modes = eigvec.shape[1]
    atom_count = lax.axis_size(ATOMS)
    atom_rank = lax.axis_index(ATOMS)
    group_rank = lax.axis_index("modes")
    total_blocks = local_blocks * atom_count
    near_blocks = min(REACH, local_blocks)
    extra_blocks = REACH - near_blocks
    extended = with_halo(eigvec, ((ATOMS, 0),), near_blocks * block_width)
    far_pieces = []
    slab_rows = eigvec.shape[0]
    for distance, far_rows in (
        (2, eigvec[slab_rows - extra_blocks * block_width :]),
        (-2, eigvec[: extra_blocks * block_width]),
    ):
        far_pieces.append(from_behind(far_rows, ATOMS, distance))
    extended = jnp.concatenate([far_pieces[0], extended, far_pieces[1]], axis=0)
    ext_blocks = extended.reshape(-1, block_width, own_modes)
    offsets = (column_blocks - atom_rank * local_blocks + REACH) % total_blocks
    picked = ext_blocks[offsets]
    masked = jnp.where(
        block_mask[:, :, None, None] > 0, operator_blocks, jnp.zeros((), operator_blocks.dtype)
    )
    product = jnp.einsum("bsij,bsjm->bim", masked, picked, preferred_element_type=jnp.float32)
    velocity = product.reshape(-1, own_modes).astype(jnp.bfloat16)
    contract = (((0,), (0,)), ((), ()))
    stacked = jnp.stack((eigvec, velocity))
    piece = lax.all_gather(stacked, "modes", axis=2, tiled=True)
    direct = lax.dot_general(eigvec, piece[1], contract, preferred_element_type=jnp.float32)
    mirror = lax.dot_general(velocity, piece[0], contract, preferred_element_type=jnp.float32)
    partial_flux = direct - mirror
    frequency = spectrum[mode_index]
    mode_total = frequency.shape[0]
    row_freq = lax.dynamic_slice_in_dim(frequency, group_rank * own_modes, own_modes)
    row_width = lax.dynamic_slice_in_dim(linewidth, group_rank * own_modes, own_modes)
    flux_tiles = sum_by_axis(
        partial_flux.astype(jnp.bfloat16), ("atoms_0", ("atoms_1", "atoms_2")), 1
    )
    share_cols = flux_tiles.shape[1]
    col_freq = lax.dynamic_slice_in_dim(frequency, atom_rank * share_cols, share_cols)
    col_width = lax.dynamic_slice_in_dim(linewidth, atom_rank * share_cols, share_cols)
    weight = pair_weight(row_freq, col_freq, row_width, col_width)
    partial_sums = jnp.sum(weight * flux_tiles * flux_tiles, axis=1)
    diffusivity = over_axes(partial_sums, ATOMS) / mode_total
    return (flux_tiles, diffusivity)


def solution(mesh):
    finer = Mesh(
        mesh.devices.reshape(2, 8, 8, mesh.shape["modes"]),
        ("atoms_0", "atoms_1", "atoms_2", "modes"),
    )
    in_specs = (
        P(ATOMS, "modes"),
        P(ATOMS, None, None, None),
        P(ATOMS, None),
        P(ATOMS, None),
        P(),
        P(),
        P(),
    )
    out_specs = (P("modes", ATOMS), P("modes"))
    return jax.shard_map(body, mesh=finer, in_specs=in_specs, out_specs=out_specs, check_vma=False)
```

profile of v0, /device:TPU:8, one launch (start us, length us, event | category | flops | bytes accessed | tf_op | source)
XLA Modules:
  0.0 219.1 jit_solution(1590429353365502931)
XLA Ops:
  7.2 3.6 %collective-permute-start.1 = (bf16[384,512]{1,0:T(8,128)(2,1)}, bf16[384,512]{1,0:T(8,128)(2,1)S(1)}, u32[]{:S(2)}, u32[]{:S(2)}) collective-permute-start(bf16[384,512]{1,0:T(8,128)(2,1)} %param.7), channel_id=1, source_target_pairs={{0,4},{4,8},{8,12},{12,16},{16,20},{20,24},{24,28},{28,32},{32,36}... | collective-permute-start | bytes 1179656 | tf_op jit(solution)/shard_map/ppermute | solution.py:19
  10.8 6.1 %collective-permute-start.2 = (bf16[384,512]{1,0:T(8,128)(2,1)}, bf16[384,512]{1,0:T(8,128)(2,1)S(1)}, u32[]{:S(2)}, u32[]{:S(2)}) collective-permute-start(bf16[384,512]{1,0:T(8,128)(2,1)} %param.7), channel_id=1, source_target_pairs={{4,0},{8,4},{12,8},{16,12},{20,16},{24,20},{28,24},{32,28},{36,32}... | collective-permute-start | bytes 1179656 | tf_op jit(solution)/shard_map/ppermute | solution.py:22
  17.0 1.0 fusion.9
  18.0 1.9 collective-permute-start
  19.9 12.4 %collective-permute-start.3 = (bf16[128,512]{1,0:T(8,128)(2,1)S(1)}, bf16[128,512]{1,0:T(8,128)(2,1)S(1)}, u32[]{:S(2)}, u32[]{:S(2)}) collective-permute-start(bf16[128,512]{1,0:T(8,128)(2,1)S(1)} %get-tuple-element.4), channel_id=1, source_target_pairs={{0,504},{4,508},{8,0},{12,4},{16,8},{20,12},{24,16},{28,20},{32,24... | collective-permute-start | bytes 393224 | tf_op jit(solution)/shard_map/ppermute | solution.py:29
  33.8 2.0 collective-permute-done
  35.8 1.0 constant_dynamic-update-slice_fusion.2
  37.1 1.1 copy-done.1
  38.2 2.1 gather_fusion
  40.3 1.8 fusion.2
  42.9 0.9 pad_maximum_fusion
  43.9 44.1 %all-gather.2.cloned.1.call-done = bf16[2,384,2048]{2,1,0:T(8,128)(2,1)} async-done(((bf16[2,384,512]{2,1,0:T(8,128)(2,1)}), bf16[2,384,2048]{2,1,0:T(8,128)(2,1)}) %all-gather.2.cloned.1.call-update) | async-done | bytes 3145744 | tf_op jit(solution)/shard_map/all_gather | solution.py:92
  88.0 2.9 %fusion.1 = f32[2048,512]{1,0:T(8,128)S(1)} fusion(bf16[384,512]{1,0:T(8,128)(2,1)S(1)} %copy-done.3, bf16[2,384,2048]{2,1,0:T(8,128)(2,1)} %all-gather.2.cloned.1.call-done), kind=kOutput, calls=%fused_computation.6 | convolution fusion | flops 805306368 | bytes 6160384 | tf_op jit(solution)/shard_map/dot_general | solution.py:93
  90.9 1.4 fusion
  92.3 1.5 copy.14
  93.8 13.5 %all-to-all-start = ((bf16[64,2,512,16]{2,3,1,0:T(8,128)(2,1)}), bf16[64,2,512,16]{2,3,1,0:T(8,128)(2,1)S(1)}, u32[]{:S(2)}, u32[]{:S(2)}) async-start(bf16[64,2,512,16]{2,3,1,0:T(8,128)(2,1)} %copy.14), calls=%async_computation | async-start | bytes 4194304 | tf_op jit(solution)/shard_map/all_to_all | solution.py:39
  107.3 11.8 %gather_fusion.1 = f32[2048]{0:T(1024)S(1)} fusion(f32[49152]{0:T(1024)S(1)} %copy-done, s32[2048]{0:T(1024)S(1)} %fusion.7), kind=kCustom, calls=%fused_computation.1 | custom fusion | bytes 24576 | tf_op jit(solution)/shard_map/gather | solution.py:96
  119.1 42.3 %all-to-all-done = bf16[64,2,512,16]{2,3,1,0:T(8,128)(2,1)S(1)} async-done(((bf16[64,2,512,16]{2,3,1,0:T(8,128)(2,1)}), bf16[64,2,512,16]{2,3,1,0:T(8,128)(2,1)S(1)}, u32[]{:S(2)}, u32[]{:S(2)}) %all-to-all-start) | async-done | bytes 2097184 | tf_op jit(solution)/shard_map/all_to_all | solution.py:39
  161.4 1.0 reduce_sum.30
  162.4 3.6 %all-to-all-start.1 = ((bf16[2,512,16]{1,2,0:T(8,128)(2,1)}), bf16[2,512,16]{1,2,0:T(8,128)(2,1)S(1)}, u32[]{:S(2)}, u32[]{:S(2)}) async-start(bf16[2,512,16]{1,2,0:T(8,128)(2,1)} %reduce_sum.30), calls=%async_computation.1 | async-start | bytes 65536 | tf_op jit(solution)/shard_map/all_to_all | solution.py:47
  167.7 3.8 %all-to-all-done.1 = bf16[2,512,16]{1,2,0:T(8,128)(2,1)S(1)} async-done(((bf16[2,512,16]{1,2,0:T(8,128)(2,1)}), bf16[2,512,16]{1,2,0:T(8,128)(2,1)S(1)}, u32[]{:S(2)}, u32[]{:S(2)}) %all-to-all-start.1) | async-done | bytes 32800 | tf_op jit(solution)/shard_map/all_to_all | solution.py:47
  171.6 6.4 %psum.21 = f32[512]{0:T(512)S(1)} all-reduce(f32[512]{0:T(512)S(1)} %fusion.6), channel_id=1, replica_groups=mesh['atoms_0'=2,'atoms_1'=8,'atoms_2'=8,'modes'=4] {'atoms_0'}, use_global_device_ids=true, to_apply=%region_3.4 | all-reduce | flops 512 | bytes 4096 | tf_op jit(solution)/shard_map/psum | solution.py:52
  178.0 15.7 %psum.22 = f32[512]{0:T(512)S(1)} all-reduce(f32[512]{0:T(512)S(1)} %psum.21), channel_id=1, replica_groups=mesh['atoms_0'=2,'atoms_1'=8,'atoms_2'=8,'modes'=4] {'atoms_1'}, use_global_device_ids=true, to_apply=%region_4.5 | all-reduce | flops 512 | bytes 4096 | tf_op jit(solution)/shard_map/psum | solution.py:52
  193.7 18.0 %psum.23 = f32[512]{0:T(512)S(1)} all-reduce(f32[512]{0:T(512)S(1)} %psum.22), channel_id=1, replica_groups=mesh['atoms_0'=2,'atoms_1'=8,'atoms_2'=8,'modes'=4] {'atoms_2'}, use_global_device_ids=true, to_apply=%region_5.6 | all-reduce | flops 512 | bytes 4096 | tf_op jit(solution)/shard_map/psum | solution.py:52
  (38 shorter events, 4.9 us)
Async XLA Ops:
  7.2 100.1 %copy-start = (f32[49152]{0:T(1024)S(1)}, f32[49152]{0:T(1024)}, u32[]{:S(2)}) copy-start(f32[49152]{0:T(1024)} %param.11) | copy-start | bytes 589828
  7.2 80.8 %all-gather.2.cloned.1.call-start = ((), (), s32[]{:S(2)}) async-start(), calls=%async_computation.2 | async-start | bytes 3932160 | tf_op jit(solution)/shard_map/all_gather | solution.py:92
  7.2 28.6 %collective-permute-start.1 = (bf16[384,512]{1,0:T(8,128)(2,1)}, bf16[384,512]{1,0:T(8,128)(2,1)S(1)}, u32[]{:S(2)}, u32[]{:S(2)}) collective-permute-start(bf16[384,512]{1,0:T(8,128)(2,1)} %param.7), channel_id=1, source_target_pairs={{0,4},{4,8},{8,12},{12,16},{16,20},{20,24},{24,28},{28,32},{32,36}... | collective-permute-start | bytes 1179656 | tf_op jit(solution)/shard_map/ppermute | solution.py:19
  10.8 26.0 %collective-permute-start.2 = (bf16[384,512]{1,0:T(8,128)(2,1)}, bf16[384,512]{1,0:T(8,128)(2,1)S(1)}, u32[]{:S(2)}, u32[]{:S(2)}) collective-permute-start(bf16[384,512]{1,0:T(8,128)(2,1)} %param.7), channel_id=1, source_target_pairs={{4,0},{8,4},{12,8},{16,12},{20,16},{24,20},{28,24},{32,28},{36,32}... | collective-permute-start | bytes 1179656 | tf_op jit(solution)/shard_map/ppermute | solution.py:22
  18.0 17.8 %collective-permute-start = (bf16[128,512]{1,0:T(8,128)(2,1)S(1)}, bf16[128,512]{1,0:T(8,128)(2,1)S(1)}, u32[]{:S(2)}, u32[]{:S(2)}) collective-permute-start(bf16[128,512]{1,0:T(8,128)(2,1)S(1)} %get-tuple-element.5), channel_id=1, source_target_pairs={{0,8},{4,12},{8,16},{12,20},{16,24},{20,28},{24,32},{28,36},{32,40... | collective-permute-start | bytes 393224 | tf_op jit(solution)/shard_map/ppermute | solution.py:29
  19.9 17.1 %collective-permute-start.3 = (bf16[128,512]{1,0:T(8,128)(2,1)S(1)}, bf16[128,512]{1,0:T(8,128)(2,1)S(1)}, u32[]{:S(2)}, u32[]{:S(2)}) collective-permute-start(bf16[128,512]{1,0:T(8,128)(2,1)S(1)} %get-tuple-element.4), channel_id=1, source_target_pairs={{0,504},{4,508},{8,0},{12,4},{16,8},{20,12},{24,16},{28,20},{32,24... | collective-permute-start | bytes 393224 | tf_op jit(solution)/shard_map/ppermute | solution.py:29
  37.1 1.1 copy-start.1
  40.3 2.6 %copy-start.2 = (bf16[384,512]{1,0:T(8,128)(2,1)S(1)}, bf16[384,512]{1,0:T(8,128)(2,1)}, u32[]{:S(2)}) copy-start(bf16[384,512]{1,0:T(8,128)(2,1)} %param.7) | copy-start | bytes 1179652
  42.1 0.7 copy-start.5
  42.1 45.9 %copy-start.3 = (bf16[384,512]{1,0:T(8,128)(2,1)S(1)}, bf16[384,512]{1,0:T(8,128)(2,1)}, u32[]{:S(2)}) copy-start(bf16[384,512]{1,0:T(8,128)(2,1)} %param.7) | copy-start | bytes 1179652
  43.9 47.0 %copy-start.6 = (bf16[3,128,512]{2,1,0:T(8,128)(2,1)S(1)}, bf16[3,128,512]{2,1,0:T(8,128)(2,1)}, u32[]{:S(2)}) copy-start(bf16[3,128,512]{2,1,0:T(8,128)(2,1)} %copy-done.5) | copy-start | bytes 1179652
  88.0 2.9 %copy-start.4 = (bf16[2,384,2048]{2,1,0:T(8,128)(2,1)S(1)}, bf16[2,384,2048]{2,1,0:T(8,128)(2,1)}, u32[]{:S(2)}) copy-start(bf16[2,384,2048]{2,1,0:T(8,128)(2,1)} %all-gather.2.cloned.1.call-done) | copy-start | bytes 9437188
  93.8 13.5 %copy-start.8 = (s32[2048]{0:T(1024)S(1)}, s32[2048]{0:T(1024)}, u32[]{:S(2)}) copy-start(s32[2048]{0:T(1024)} %param.12) | copy-start | bytes 24580
  93.8 67.6 %all-to-all-start = ((bf16[64,2,512,16]{2,3,1,0:T(8,128)(2,1)}), bf16[64,2,512,16]{2,3,1,0:T(8,128)(2,1)S(1)}, u32[]{:S(2)}, u32[]{:S(2)}) async-start(bf16[64,2,512,16]{2,3,1,0:T(8,128)(2,1)} %copy.14), calls=%async_computation | async-start | bytes 4194304 | tf_op jit(solution)/shard_map/all_to_all | solution.py:39
  162.4 9.1 %all-to-all-start.1 = ((bf16[2,512,16]{1,2,0:T(8,128)(2,1)}), bf16[2,512,16]{1,2,0:T(8,128)(2,1)S(1)}, u32[]{:S(2)}, u32[]{:S(2)}) async-start(bf16[2,512,16]{1,2,0:T(8,128)(2,1)} %reduce_sum.30), calls=%async_computation.1 | async-start | bytes 65536 | tf_op jit(solution)/shard_map/all_to_all | solution.py:47
  171.5 40.8 %copy-start.7 = (f32[512,16]{0,1:T(8,128)}, f32[512,16]{0,1:T(8,128)S(1)}, u32[]{:S(2)}) copy-start(f32[512,16]{0,1:T(8,128)S(1)} %convert_reduce_fusion) | copy-start | bytes 98308
Sparse Core Ops, SparseCore 0:
  44.0 43.9 all-gather.1
where the time goes:
time: 220 us; the launch traced here: 219 us
  waiting for transfers between devices  92.4 us (42%)
  starting transfers between devices  41.3 us (19%)
  blocking collectives  40.1 us (18%)
  local copies, waits for them, and re-layouts  21 us (10%)
  between operations  14.3 us (6%)
  matrix products  6.01 us (3%)
  other arithmetic  4.09 us (2%)
    all_gather x1, waiting for transfers between devices, body(): piece = lax.all_gather(stacked, 'modes', axis=2, tiled=True)  44.1 us
    all_to_all x1, waiting for transfers between devices, sent_and_summed(): lax.all_to_all(pieces, axis, split_axis=0, concat_axis=0, tiled=True)  42.3 us
    psum x3, blocking collectives, over_axes(): return functools.reduce(lax.psum, axes, value)  40.1 us
    ppermute x2, starting transfers between devices, from_behind(): lax.ppermute(value, axis, [(i, (i + by) % devices) for i in range(devices)])  14.3 us
    all_to_all x1, starting transfers between devices, sent_and_summed(): lax.all_to_all(pieces, axis, split_axis=0, concat_axis=0, tiled=True)  13.5 us
    gather x1, local copies, waits for them, and re-layouts, body(): frequency = spectrum[mode_index]  11.8 us
    ppermute x1, starting transfers between devices, with_halo(): lax.ppermute(lax.slice_in_dim(block, 0, width, axis=dim), axis, backward)  6.14 us
  transfers between devices with their start and end apart: 7, of which 5 were waited for; matrix products, arithmetic and copies ran while one was open for 8% of the time, Pallas kernels for 0%

commit v1 on v0

v1 whole, which is shorter than its diff:
```python
import functools

import jax
import jax.numpy as jnp
from jax import lax
from jax.experimental import pallas as pl
from jax.experimental.pallas import tpu as pltpu
from jax.sharding import PartitionSpec as P

BF = jnp.bfloat16
F32 = jnp.float32
NX, NZ, NY = 2, 8, 8
ATOMS = NX * NZ * NY
REACH = 4
BAND = 2 * REACH + 1
BS = 128
LB = 3
UP = ((0, 7), (0, 8), (1, 6), (1, 7), (1, 8), (2, 5), (2, 6), (2, 7), (2, 8))
DOWN = ((0, 1), (0, 2), (0, 3), (1, 0), (1, 1), (1, 2), (2, 0), (2, 1), (0, 0))


def kernel(
    e_hbm, op_hbm, col_s, mask_s, spec_ref, midx_ref, width_ref,
    tile_ref, diff_ref,
    ext, others, turned, opv, dense, up_send, dn_send, lo_blk, hi_blk, lo_far, hi_far,
    bmat, wmat, pz, py, rz_plus, rz_minus, ry_plus, ry_minus, z_mid, y_mid, z_in, y_in,
    s_y, s_xz,
    load_sem, halo_send, halo_recv, mode_send, mode_recv, blk_send, blk_recv,
    ring_send, ring_recv, far_send, far_recv, sum_send, sum_recv,
):
    me = lax.axis_index("atoms")
    mode = lax.axis_index("modes")
    x_lo, core = mode // 2, mode % 2
    x, z, y = me // (NZ * NY), (me // NY) % NZ, me % NY
    above = ((me + 1) % ATOMS, mode)
    below = ((me + ATOMS - 1) % ATOMS, mode)
    twin = (me, x_lo * 2 + 1 - core)
    across = (me, (1 - x_lo) * 2 + core)
    twin_mode = x_lo * 2 + 1 - core
    across_mode = (1 - x_lo) * 2 + core
    last_mode = (1 - x_lo) * 2 + 1 - core

    def at_y(o):
        return (x * (NZ * NY) + z * NY + (y + o) % NY, mode)

    def at_z(o):
        return (x * (NZ * NY) + ((z + o) % NZ) * NY + y, mode)

    gz = x * NZ + z
    gy = x * NY + y

    def group_xz(o):
        g = (gz + o) % 16
        return g, (g * NY + y, mode)

    def group_xy(o):
        g = (gy + o) % 16
        return g, ((g // NY) * (NZ * NY) + z * NY + g % NY, mode)

    def remote(src, dst, ssem, rsem, device):
        return pltpu.make_async_remote_copy(
            src_ref=src, dst_ref=dst, send_sem=ssem, recv_sem=rsem,
            device_id=device, device_id_type=pl.DeviceIdType.MESH,
        )

    barrier = pltpu.get_barrier_semaphore()

    def greet(device):
        pl.semaphore_signal(
            barrier, inc=1, device_id=device, device_id_type=pl.DeviceIdType.MESH
        )

    for device in (above, below, twin, across):
        greet(device)

    def greet_far(o, carry):
        greet(group_xz(o)[1])
        greet(group_xy(o)[1])
        return carry

    lax.fori_loop(1, 16, greet_far, 0)

    load_op = pltpu.make_async_copy(op_hbm, opv, load_sem.at[0])
    load_op.start()
    load_e = [
        pltpu.make_async_copy(e_hbm.at[pl.ds(b * BS, BS)], ext.at[REACH + b], load_sem.at[1 + b])
        for b in range(LB)
    ]
    for copy in load_e:
        copy.start()

    load_op.wait()
    for r in range(LB):
        for d in range(BAND):
            target = (me * LB + r + d - REACH + ATOMS * LB) % (ATOMS * LB)
            slot = jnp.int32(0)
            used = jnp.int32(0)
            for s in range(8):
                hit = col_s[r, s] == target
                slot = jnp.where(hit, s, slot)
                used = jnp.where(hit, mask_s[r, s], used)
            keep = jnp.where(used > 0, F32(1), F32(0)).astype(F32)
            block = (opv[r, slot].astype(F32) * keep).astype(BF)
            dense[r, d] = block
            if (r, d) in UP:
                up_send[UP.index((r, d))] = block
            if (r, d) in DOWN:
                dn_send[DOWN.index((r, d))] = block
    up_send[9] = jnp.zeros((BS, BS), BF)
    dn_send[9] = jnp.zeros((BS, BS), BF)

    pl.semaphore_wait(barrier, 34)

    sends = []

    def go(*args):
        copy = remote(*args)
        copy.start()
        sends.append(copy)
        return copy

    go(e_hbm, others.at[0], mode_send.at[0], mode_recv.at[0], across)
    go(e_hbm, others.at[1], mode_send.at[1], mode_recv.at[1], twin)
    half = pl.ds(core * 5, 5)
    go(up_send.at[half], lo_blk.at[half], blk_send.at[0], blk_recv.at[0], above)
    go(dn_send.at[half], hi_blk.at[half], blk_send.at[1], blk_recv.at[1], below)
    for b in (2, 1, 0):
        go(e_hbm.at[pl.ds(b * BS, BS)], ext.at[1 + b], halo_send.at[b], halo_recv.at[b], above)
        t = 2 - b
        go(e_hbm.at[pl.ds(t * BS, BS)], ext.at[7 + t], halo_send.at[3 + t], halo_recv.at[3 + t], below)

    def arrived(dst, sem):
        remote(dst, dst, sem, sem, above).wait_recv()

    arrived(ext.at[3], halo_recv.at[2])
    go(ext.at[3], ext.at[0], halo_send.at[6], halo_recv.at[6], above)
    arrived(ext.at[7], halo_recv.at[3])
    go(ext.at[7], ext.at[10], halo_send.at[7], halo_recv.at[7], below)

    arrived(lo_blk.at[half], blk_recv.at[0])
    go(lo_blk.at[half], lo_blk.at[half], blk_send.at[2], blk_recv.at[2], twin)
    arrived(hi_blk.at[half], blk_recv.at[1])
    go(hi_blk.at[half], hi_blk.at[half], blk_send.at[3], blk_recv.at[3], twin)
    other_half = pl.ds((1 - core) * 5, 5)
    arrived(lo_blk.at[other_half], blk_recv.at[2])
    go(lo_blk.at[8], lo_far, blk_send.at[4], blk_recv.at[4], above)
    arrived(hi_blk.at[other_half], blk_recv.at[3])
    go(hi_blk.at[8], hi_far, blk_send.at[5], blk_recv.at[5], below)

    def build(r, d, mirror):
        value = mirror.astype(F32).T - dense[r, d].astype(F32)
        bmat[r, :, d * BS : (d + 1) * BS] = value.astype(BF)

    for r in range(LB):
        for c in range(LB):
            d = c - r + REACH
            build(r, d, dense[c, 2 * REACH - d])
    for k in range(8):
        c, d = UP[k]
        r = d + c - 7
        build(r, c + 1 - r, lo_blk[k])
        c, d = DOWN[k]
        r = d + c - 1
        build(r, c + 7 - r, hi_blk[k])

    def turn(slot_mode, get):
        for b in range(LB):
            turned[slot_mode, :, b * BS : (b + 1) * BS] = get(b).T

    for copy in load_e:
        copy.wait()
    turn(mode, lambda b: ext[REACH + b])
    arrived(others.at[1], mode_recv.at[1])
    turn(twin_mode, lambda b: others[1, b * BS : (b + 1) * BS, :])
    arrived(others.at[0], mode_recv.at[0])
    go(others.at[0], others.at[2], mode_send.at[2], mode_recv.at[2], twin)
    turn(across_mode, lambda b: others[0, b * BS : (b + 1) * BS, :])
    arrived(others.at[2], mode_recv.at[2])
    turn(last_mode, lambda b: others[2, b * BS : (b + 1) * BS, :])

    arrived(lo_far, blk_recv.at[4])
    build(0, 0, lo_far[...])
    arrived(hi_far, blk_recv.at[5])
    build(2, 8, hi_far[...])
    for index, sem in ((1, 0), (2, 1), (8, 4), (9, 5), (0, 6), (10, 7)):
        arrived(ext.at[index], halo_recv.at[sem])

    for r in range(LB):
        rows = ext[r : r + BAND].reshape(BAND * BS, 512)
        wmat[r * BS : (r + 1) * BS, :] = jnp.dot(
            bmat[r], rows, preferred_element_type=F32
        ).astype(BF)

    def product(mb, carry):
        part = jnp.dot(turned[mb], wmat[...], preferred_element_type=F32).astype(BF)
        for q in range(4):
            rows = part[q * BS : (q + 1) * BS]
            pz[(mb % 2) * 4 + q, pl.ds((mb // 2) * NY, NY)] = rows[:, :256].reshape(NY, 16, 256)
            py[:, mb * 4 + q] = rows[:, 256:].reshape(NY, 16, 256)
        return carry

    lax.fori_loop(0, 4, product, 0)

    A, B = 0, 1

    def index(sense, h, k):
        long = (h == A) if sense == 0 else (h == B)
        return 4 - k if long else 7 - k

    rings = (
        (pz, (rz_plus, rz_minus), z, (at_z(1), at_z(NZ - 1)), 0),
        (py, (ry_plus, ry_minus), y, (at_y(1), at_y(NY - 1)), 1),
    )

    def hand(ring, sense, h, k, src):
        _, recv, _, devices, r = ring
        i = index(sense, h, k)
        go(src, recv[sense].at[i], ring_send.at[r, sense, i], ring_recv.at[r, sense, i], devices[sense])

    def owner(ring, sense, k):
        return (ring[2] + (k if sense == 0 else 8 - k)) % 8

    for sense, h, k in ((0, A, 4), (1, B, 4), (0, B, 3), (1, A, 3)):
        for ring in rings:
            hand(ring, sense, h, k, ring[0].at[owner(ring, sense, k), pl.ds(h * 8, 8)])

    def take(ring, sense, h, k):
        i = index(sense, h, k)
        arrived(ring[1][sense].at[i], ring_recv.at[ring[4], sense, i])
        return i

    for k in (4, 3, 2):
        for sense, h, kk in ((0, A, k), (1, B, k), (0, B, k - 1), (1, A, k - 1)):
            if kk < 2:
                continue
            for ring in rings:
                i = take(ring, sense, h, kk)
                buf = ring[1][sense]
                mine = ring[0][owner(ring, sense, kk - 1), h * 8 : h * 8 + 8]
                buf[i] = (buf[i].astype(F32) + mine.astype(F32)).astype(BF)
                hand(ring, sense, h, kk - 1, buf.at[i])
    for h in (A, B):
        for ring, mid in zip(rings, (z_mid, y_mid)):
            i = take(ring, 0, h, 1)
            j = take(ring, 1, h, 1)
            mine = ring[0][ring[2], h * 8 : h * 8 + 8]
            mid[h * 8 : h * 8 + 8] = (
                mine.astype(F32) + ring[1][0][i].astype(F32) + ring[1][1][j].astype(F32)
            ).astype(BF)

    def direct_z(o):
        g, device = group_xy(o)
        return remote(z_mid.at[g], z_in.at[gy], far_send.at[0, g], far_recv.at[0, gy], device)

    def direct_y(o):
        g, device = group_xz(o)
        return remote(y_mid.at[g], y_in.at[gz], far_send.at[1, g], far_recv.at[1, gz], device)

    def send_direct(o, carry):
        direct_z(o).start()
        direct_y(o).start()
        return carry

    lax.fori_loop(1, 16, send_direct, 0)
    z_in[gy] = z_mid[gy]
    y_in[gz] = y_mid[gz]

    spot = lax.broadcasted_iota(jnp.int32, (16, 512), 0) + (me % 32) * 16
    on_tile = lax.broadcasted_iota(jnp.int32, (16, 512), 1) == spot

    def column(row):
        spread = jnp.where(on_tile, jnp.broadcast_to(row, (16, 512)), F32(0))
        return jnp.sum(spread, axis=1, keepdims=True)

    def frequency(block):
        at = midx_ref[block]
        high = lax.broadcasted_iota(jnp.int32, (384, 512), 0) == jnp.broadcast_to(at // 128, (384, 512))
        rows = lax.dot_general(
            spec_ref[...], high.astype(F32), (((0,), (0,)), ((), ())),
            precision=lax.Precision.HIGHEST, preferred_element_type=F32,
        )
        low = lax.broadcasted_iota(jnp.int32, (128, 512), 0) == jnp.broadcast_to(at % 128, (128, 512))
        return jnp.sum(jnp.where(low, rows, F32(0)), axis=0, keepdims=True)

    row_freq = frequency(mode)
    row_width = width_ref[mode]
    col_freq = column(frequency(me // 32))
    col_width = column(width_ref[me // 32])
    freq_sum = row_freq + col_freq
    spacing = row_freq - col_freq
    mean_width = 0.5 * (row_width + col_width)
    factor = freq_sum * freq_sum / (4.0 * row_freq * col_freq)
    weight = factor * mean_width / (spacing * spacing + mean_width * mean_width)

    def wait_direct(o, carry):
        g = (gy + o) % 16
        arrived(z_in.at[g], far_recv.at[0, g])
        g = (gz + o) % 16
        arrived(y_in.at[g], far_recv.at[1, g])
        return carry

    lax.fori_loop(1, 16, wait_direct, 0)
    tile = jnp.concatenate(
        [jnp.sum(z_in[...].astype(F32), axis=0), jnp.sum(y_in[...].astype(F32), axis=0)], axis=1
    )
    tile_ref[...] = tile
    share = jnp.sum(weight * tile * tile, axis=0, keepdims=True)

    def packed(slot):
        for q in range(4):
            slot[q : q + 1, :] = share[:, q * BS : (q + 1) * BS]
        slot[4:8, :] = jnp.zeros((4, BS), F32)

    packed(s_y.at[y])
    for o in range(1, NY):
        go(s_y.at[y], s_y.at[y], sum_send.at[o], sum_recv.at[y], at_y(o))

    def wait_y(o, carry):
        g = (y + o) % NY
        arrived(s_y.at[g], sum_recv.at[g])
        return carry

    lax.fori_loop(1, NY, wait_y, 0)
    s_xz[gz] = jnp.sum(s_y[...], axis=0)

    def sum_xz(o):
        return remote(
            s_xz.at[gz], s_xz.at[gz], sum_send.at[8 + o], sum_recv.at[8 + gz], group_xz(o)[1]
        )

    def send_xz(o, carry):
        sum_xz(o).start()
        return carry

    lax.fori_loop(1, 16, send_xz, 0)

    def wait_xz(o, carry):
        g = (gz + o) % 16
        arrived(s_xz.at[g], sum_recv.at[8 + g])
        return carry

    lax.fori_loop(1, 16, wait_xz, 0)
    diff_ref[...] = jnp.sum(s_xz[...], axis=0) * F32(1.0 / 2048)

    for copy in sends:
        copy.wait_send()

    def finish(o, carry):
        direct_z(o).wait_send()
        direct_y(o).wait_send()
        sum_xz(o).wait_send()
        return carry

    lax.fori_loop(1, 16, finish, 0)


def body(eigvec, operator_blocks, column_blocks, block_mask, spectrum, mode_index, linewidth):
    anywhere = pl.BlockSpec(memory_space=pl.ANY)
    scalars = pl.BlockSpec(memory_space=pltpu.SMEM)
    vmem = pl.BlockSpec(memory_space=pltpu.VMEM)
    dma = pltpu.SemaphoreType.DMA
    ring_buffer = pltpu.VMEM((7, 8, 16, 256), BF)
    tile, diff = pl.pallas_call(
        kernel,
        out_shape=(
            jax.ShapeDtypeStruct((16, 512), F32),
            jax.ShapeDtypeStruct((8, BS), F32),
        ),
        in_specs=[anywhere, anywhere, scalars, scalars, vmem, vmem, vmem],
        out_specs=(vmem, vmem),
        scratch_shapes=[
            pltpu.VMEM((11, BS, 512), BF),
            pltpu.VMEM((3, LB * BS, 512), BF),
            pltpu.VMEM((4, 512, LB * BS), BF),
            pltpu.VMEM((LB, 8, BS, BS), BF),
            pltpu.VMEM((LB, BAND, BS, BS), BF),
            pltpu.VMEM((10, BS, BS), BF),
            pltpu.VMEM((10, BS, BS), BF),
            pltpu.VMEM((10, BS, BS), BF),
            pltpu.VMEM((10, BS, BS), BF),
            pltpu.VMEM((BS, BS), BF),
            pltpu.VMEM((BS, BS), BF),
            pltpu.VMEM((LB, BS, BAND * BS), BF),
            pltpu.VMEM((LB * BS, 512), BF),
            pltpu.VMEM((NZ, 16, 16, 256), BF),
            pltpu.VMEM((NY, 16, 16, 256), BF),
            ring_buffer, ring_buffer, ring_buffer, ring_buffer,
            pltpu.VMEM((16, 16, 256), BF),
            pltpu.VMEM((16, 16, 256), BF),
            pltpu.VMEM((16, 16, 256), BF),
            pltpu.VMEM((16, 16, 256), BF),
            pltpu.VMEM((NY, 8, BS), F32),
            pltpu.VMEM((16, 8, BS), F32),
            dma((4,)), dma((8,)), dma((8,)), dma((3,)), dma((3,)), dma((6,)), dma((6,)),
            dma((2, 2, 7)), dma((2, 2, 7)), dma((2, 16)), dma((2, 16)), dma((24,)), dma((24,)),
        ],
        compiler_params=pltpu.CompilerParams(
            collective_id=0, has_side_effects=True, vmem_limit_bytes=40 * 1024 * 1024
        ),
    )(
        eigvec, operator_blocks, column_blocks, block_mask,
        spectrum.reshape(384, 128), mode_index.reshape(4, 1, 512), linewidth.reshape(4, 1, 512),
    )
    return tile.T, diff[:4].reshape(512)


def solution(mesh):
    in_specs = (
        P("atoms", "modes"),
        P("atoms", None, None, None),
        P("atoms", None),
        P("atoms", None),
        P(),
        P(),
        P(),
    )
    out_specs = (P("modes", "atoms"), P("modes"))
    return jax.shard_map(body, mesh=mesh, in_specs=in_specs, out_specs=out_specs, check_vma=False)
```

time: 220 us -> 87.2 us (0.40)
  the two profiles are of different devices: /device:TPU:8 before, /device:TPU:2 now
where the time goes in v1:
time: 87.2 us; the launch traced here: 86.8 us
  Pallas kernels  79.9 us (92%)
  local copies, waits for them, and re-layouts  6.32 us (7%)
    pallas_call x1, Pallas kernels, body(): pl.pallas_call(kernel, out_shape=(jax.ShapeDtypeStruct((16, 512), F32), j...  79.9 us
    unnamed x15, local copies, waits for them, and re-layouts  5.74 us

profile of v1, /device:TPU:2, one launch (start us, length us, event | category | flops | bytes accessed | tf_op | source)
XLA Modules:
  0.0 86.8 jit_solution(6516988389643732180)
XLA Ops:
  0.6 0.0 copy-start.6
  0.6 0.0 copy-start.5
  0.7 0.7 copy-done.6
  1.3 0.0 copy-done.5
  1.3 0.0 copy-start
  1.3 1.1 %copy-done = bf16[3,8,128,128]{3,2,1,0:T(8,128)(2,1)S(1)} copy-done((bf16[3,8,128,128]{3,2,1,0:T(8,128)(2,1)S(1)}, bf16[3,8,128,128]{3,2,1,0:T(8,128)(2,1)}, u32[]{:S(2)}) %copy-start) | copy-done | bytes 786456
  2.5 0.0 copy-start.1
  2.5 1.0 %copy-done.1 = bf16[384,512]{1,0:T(8,128)(2,1)S(1)} copy-done((bf16[384,512]{1,0:T(8,128)(2,1)S(1)}, bf16[384,512]{1,0:T(8,128)(2,1)}, u32[]{:S(2)}) %copy-start.1) | copy-done | bytes 393240
  3.5 0.0 copy-start.2
  3.5 0.9 %copy-done.2 = f32[49152]{0:T(1024)S(1)} copy-done((f32[49152]{0:T(1024)S(1)}, f32[49152]{0:T(1024)}, u32[]{:S(2)}) %copy-start.2) | copy-done | bytes 196632
  4.4 0.0 copy-start.3
  4.4 0.7 copy-done.3
  5.1 0.0 copy-start.4
  5.1 0.7 copy-done.4
  5.8 79.9 %shard_map.86 = (f32[16,512]{1,0:T(8,128)S(1)}, f32[8,128]{1,0:T(8,128)S(1)}) custom-call(bf16[384,512]{1,0:T(8,128)(2,1)S(1)} %copy-done.1, bf16[3,8,128,128]{3,2,1,0:T(8,128)(2,1)S(1)} %copy-done, s32[3,8]{1,0:T(4,128)S(1)} %copy-done.5, s32[3,8]{1,0:T(4,128)S(1)} %copy-done.6, f32[384,128]{1,0:T(8,128)S(1)} %bitcast.6, s32[4,1,512]{2,1,0:T(1,128)S(1)} %bitcast.8, ...), custom_call_target="tpu_custom_call" | custom-call | tf_op jit(solution)/shard_map/pallas_call | solution.py:363
  85.6 0.6 slice_bitcast_fusion
  86.2 0.6 copy.10
Async XLA Ops:
  0.6 0.7 copy-start.6
  0.6 0.7 copy-start.5
  1.3 1.1 %copy-start = (bf16[3,8,128,128]{3,2,1,0:T(8,128)(2,1)S(1)}, bf16[3,8,128,128]{3,2,1,0:T(8,128)(2,1)}, u32[]{:S(2)}) copy-start(bf16[3,8,128,128]{3,2,1,0:T(8,128)(2,1)} %op_hbm.1) | copy-start | bytes 2359300
  2.5 1.0 %copy-start.1 = (bf16[384,512]{1,0:T(8,128)(2,1)S(1)}, bf16[384,512]{1,0:T(8,128)(2,1)}, u32[]{:S(2)}) copy-start(bf16[384,512]{1,0:T(8,128)(2,1)} %e_hbm.1) | copy-start | bytes 1179652
  3.5 0.9 %copy-start.2 = (f32[49152]{0:T(1024)S(1)}, f32[49152]{0:T(1024)}, u32[]{:S(2)}) copy-start(f32[49152]{0:T(1024)} %param.11) | copy-start | bytes 589828
  4.4 0.7 copy-start.3
  5.1 0.7 copy-start.4

commit v2 on v1

v2 whole, which is shorter than its diff:
```python
import functools

import jax
import jax.numpy as jnp
from jax import lax
from jax.experimental import pallas as pl
from jax.experimental.pallas import tpu as pltpu
from jax.sharding import PartitionSpec as P

BF = jnp.bfloat16
F32 = jnp.float32
NX, NZ, NY = 2, 8, 8
ATOMS = NX * NZ * NY
REACH = 4
BAND = 2 * REACH + 1
BS = 128
LB = 3
UP = ((0, 7), (0, 8), (1, 6), (1, 7), (1, 8), (2, 5), (2, 6), (2, 7), (2, 8))
DOWN = ((0, 1), (0, 2), (0, 3), (1, 0), (1, 1), (1, 2), (2, 0), (2, 1), (0, 0))


def kernel(
    e_hbm, op_hbm, col_hbm, mask_hbm, spec_hbm, midx_hbm, width_hbm,
    tile_ref, diff_ref,
    ext, others, turned, opv, col_s, mask_s, spec_ref, midx_ref, width_ref,
    dense, up_send, dn_send, lo_blk, hi_blk, lo_far, hi_far,
    bmat, wmat, pz, py, rz_plus, rz_minus, ry_plus, ry_minus, z_mid, y_mid, z_in, y_in,
    s_y, s_xz,
    load_sem, mode_send, mode_recv, blk_send, blk_recv, msg_send, msg_recv,
    ring_send, ring_recv, far_send, far_recv, sum_send, sum_recv,
):
    me = lax.axis_index("atoms")
    mode = lax.axis_index("modes")
    x_lo, core = mode // 2, mode % 2
    x, z, y = me // (NZ * NY), (me // NY) % NZ, me % NY
    above = ((me + 1) % ATOMS, mode)
    below = ((me + ATOMS - 1) % ATOMS, mode)
    twin = (me, x_lo * 2 + 1 - core)
    across = (me, (1 - x_lo) * 2 + core)
    twin_mode = x_lo * 2 + 1 - core
    across_mode = (1 - x_lo) * 2 + core
    last_mode = (1 - x_lo) * 2 + 1 - core

    def at_y(o):
        return (x * (NZ * NY) + z * NY + (y + o) % NY, mode)

    def at_z(o):
        return (x * (NZ * NY) + ((z + o) % NZ) * NY + y, mode)

    gz = x * NZ + z
    gy = x * NY + y

    def group_xz(o):
        g = (gz + o) % 16
        return g, (g * NY + y, mode)

    def group_xy(o):
        g = (gy + o) % 16
        return g, ((g // NY) * (NZ * NY) + z * NY + g % NY, mode)

    top = (y == NY - 1) & (z == NZ - 1)
    bottom = (y == 0) & (z == 0)
    above_across = ((me + 1) % ATOMS, across_mode)
    below_across = ((me + ATOMS - 1) % ATOMS, across_mode)

    def remote(src, dst, ssem, rsem, device):
        return pltpu.make_async_remote_copy(
            src_ref=src, dst_ref=dst, send_sem=ssem, recv_sem=rsem,
            device_id=device, device_id_type=pl.DeviceIdType.MESH,
        )

    loads = (
        (op_hbm, opv), (col_hbm, col_s), (mask_hbm, mask_s),
        (e_hbm.at[:, pl.ds(0, 256)], ext.at[0, pl.ds(REACH * BS, LB * BS)]),
        (e_hbm.at[:, pl.ds(256, 256)], ext.at[1, pl.ds(REACH * BS, LB * BS)]),
        (spec_hbm, spec_ref), (midx_hbm, midx_ref), (width_hbm, width_ref),
    )
    loads = [pltpu.make_async_copy(a, b, load_sem.at[i]) for i, (a, b) in enumerate(loads)]
    for copy in loads:
        copy.start()

    barrier = pltpu.get_barrier_semaphore()

    def greet(device):
        pl.semaphore_signal(
            barrier, inc=1, device_id=device, device_id_type=pl.DeviceIdType.MESH
        )

    for device in (above, below, twin, across):
        greet(device)
    greet(((me + 2) % ATOMS, mode))
    greet(((me + ATOMS - 2) % ATOMS, mode))
    for o in range(1, 16):
        greet(group_xz(o)[1])
        greet(group_xy(o)[1])

    @pl.when(top)
    def _():
        greet(above_across)

    @pl.when(bottom)
    def _():
        greet(below_across)

    extra = jnp.where(top | bottom, 1, 0)

    for copy in loads[:3]:
        copy.wait()
    for r in range(LB):
        for d in range(BAND):
            target = (me * LB + r + d - REACH + ATOMS * LB) % (ATOMS * LB)
            slot = jnp.int32(0)
            used = jnp.int32(0)
            for s in range(8):
                hit = col_s[r, s] == target
                slot = jnp.where(hit, s, slot)
                used = jnp.where(hit, mask_s[r, s], used)
            keep = jnp.where(used > 0, F32(1), F32(0)).astype(F32)
            block = (opv[r, slot].astype(F32) * keep).astype(BF)
            dense[r, d] = block
            if (r, d) in UP:
                up_send[UP.index((r, d))] = block
            if (r, d) in DOWN:
                dn_send[DOWN.index((r, d))] = block
    up_send[9] = jnp.zeros((BS, BS), BF)
    dn_send[9] = jnp.zeros((BS, BS), BF)

    pl.semaphore_wait(barrier, 36 + extra)

    sends = []

    def go(*args):
        copy = remote(*args)
        copy.start()
        sends.append(copy)
        return copy

    def arrived(dst, sem):
        remote(dst, dst, sem, sem, above).wait_recv()

    half = pl.ds(core * 5, 5)
    other_half = pl.ds((1 - core) * 5, 5)
    messages = [[(up_send.at[half], lo_blk.at[half])], [(dn_send.at[half], hi_blk.at[half])]]
    for h in range(2):
        lanes = pl.ds(h * 256, 256)
        rows = ext.at[h]
        messages[0] += [
            (e_hbm.at[pl.ds(256, 128), lanes], rows.at[pl.ds(384, 128)]),
            (e_hbm.at[pl.ds(0, 256), lanes], rows.at[pl.ds(128, 256)]),
            (rows.at[pl.ds(384, 128)], rows.at[pl.ds(0, 128)]),
        ]
        messages[1] += [
            (e_hbm.at[pl.ds(0, 128), lanes], rows.at[pl.ds(896, 128)]),
            (e_hbm.at[pl.ds(128, 256), lanes], rows.at[pl.ds(1024, 256)]),
            (rows.at[pl.ds(896, 128)], rows.at[pl.ds(1280, 128)]),
        ]
        if h == 0:
            messages[0].append((up_send.at[8], lo_far))
            messages[1].append((dn_send.at[8], hi_far))

    def tell(way, i):
        src, dst = messages[way][i]
        atoms, edge = (above[0], top) if way == 0 else (below[0], bottom)
        to_mode = jnp.where(edge, across_mode, mode) if i == 0 else mode
        if i == 4:
            atoms = (me + (2 if way == 0 else ATOMS - 2)) % ATOMS
        copy = remote(src, dst, msg_send.at[way, i], msg_recv.at[way, i], (atoms, to_mode))
        sends.append(copy)
        if i in (1, 2, 5, 6):
            pl.when(jnp.logical_not(edge))(copy.start)
        else:
            copy.start()

    def tell_both(i):
        tell(0, i)
        tell(1, i)

    def tell_for_across(way, i):
        h = i // 4
        start, count = (((256, 128), (0, 256)) if way == 0 else ((0, 128), (128, 256)))[i % 4 - 1]
        src = others.at[0, pl.ds(start, count), pl.ds(h * 256, 256)]
        remote(
            src, messages[way][i][1], msg_send.at[way, i], msg_recv.at[way, i],
            (above_across, below_across)[way],
        ).start()

    def lanes_of(h):
        return others.at[0, :, pl.ds(h * 256, 256)]

    def gather_arrived(h):
        arrived(lanes_of(h), mode_recv.at[h])

    def relay(h):
        for way, edge in ((0, top), (1, bottom)):

            @pl.when(edge)
            def _():
                gather_arrived(h)
                tell_for_across(way, 4 * h + 1)
                tell_for_across(way, 4 * h + 2)

    def hear(way, i):
        arrived(messages[way][i][1], msg_recv.at[way, i])

    for h in range(2):
        go(e_hbm.at[:, pl.ds(h * 256, 256)], lanes_of(h), mode_send.at[h], mode_recv.at[h], across)
    go(e_hbm, others.at[1], mode_send.at[2], mode_recv.at[2], twin)
    for i in (0, 1, 2, 4, 5):
        tell_both(i)

    def turn(slot_mode, b, block):
        turned[slot_mode, :, b * BS : (b + 1) * BS] = block.T

    def build(r, d, mirror):
        value = mirror.astype(F32).T - dense[r, d].astype(F32)
        bmat[r, :, d * BS : (d + 1) * BS] = value.astype(BF)

    for copy in loads[3:]:
        copy.wait()
    for r in range(LB):
        for c in range(LB):
            d = c - r + REACH
            build(r, d, dense[c, 2 * REACH - d])
    for b in range(LB):
        for h in range(2):
            turned[mode, h * 256 : (h + 1) * 256, b * BS : (b + 1) * BS] = ext[
                h, (REACH + b) * BS : (REACH + b + 1) * BS
            ].T

    relay(0)
    hear(0, 0)
    go(lo_blk.at[half], lo_blk.at[half], blk_send.at[0], blk_recv.at[0], twin)
    hear(1, 0)
    go(hi_blk.at[half], hi_blk.at[half], blk_send.at[1], blk_recv.at[1], twin)
    hear(0, 1)
    tell(0, 3)
    hear(1, 1)
    tell(1, 3)
    tell_both(6)
    relay(1)

    arrived(lo_blk.at[other_half], blk_recv.at[0])
    arrived(hi_blk.at[other_half], blk_recv.at[1])
    for k in range(8):
        c, d = UP[k]
        r = d + c - 7
        build(r, c + 1 - r, lo_blk[k])
        c, d = DOWN[k]
        r = d + c - 1
        build(r, c + 7 - r, hi_blk[k])

    arrived(others.at[1], mode_recv.at[2])
    for b in range(LB):
        turn(twin_mode, b, others[1, b * BS : (b + 1) * BS, :])
    for h in range(2):
        pl.when(jnp.logical_not(top | bottom))(functools.partial(gather_arrived, h))
        half_lanes = pl.ds(h * 256, 256)
        go(lanes_of(h), others.at[2, :, half_lanes], mode_send.at[3 + h], mode_recv.at[3 + h], twin)
        for b in range(LB):
            turned[across_mode, h * 256 : (h + 1) * 256, b * BS : (b + 1) * BS] = others[
                0, b * BS : (b + 1) * BS, h * 256 : (h + 1) * 256
            ].T
    for h in range(2):
        arrived(others.at[2, :, pl.ds(h * 256, 256)], mode_recv.at[3 + h])
        for b in range(LB):
            turned[last_mode, h * 256 : (h + 1) * 256, b * BS : (b + 1) * BS] = others[
                2, b * BS : (b + 1) * BS, h * 256 : (h + 1) * 256
            ].T

    hear(0, 4)
    build(0, 0, lo_far[...])
    hear(1, 4)
    build(2, 8, hi_far[...])

    def apply_operator(h):
        for r in range(LB):
            wmat[h, r * BS : (r + 1) * BS, :] = jnp.dot(
                bmat[r], ext[h, r * BS : (r + BAND) * BS], preferred_element_type=F32
            ).astype(BF)

    def product(h):
        def step(mb, carry):
            part = jnp.dot(turned[mb], wmat[h], preferred_element_type=F32).astype(BF)
            for q in range(4):
                rows = part[q * BS : (q + 1) * BS].reshape(NY, 16, 256)
                if h == 0:
                    pz[(mb % 2) * 4 + q, pl.ds((mb // 2) * NY, NY)] = rows
                else:
                    py[:, mb * 4 + q] = rows
            return carry

        lax.fori_loop(0, 4, step, 0)

    def index(sense, h, k):
        long = h // 2 == sense
        return (4 - k if long else 7 - k) * 2 + h % 2

    rings = (
        (pz, (rz_plus, rz_minus), z, (at_z(1), at_z(NZ - 1)), 0),
        (py, (ry_plus, ry_minus), y, (at_y(1), at_y(NY - 1)), 1),
    )

    def hand(ring, sense, h, k, src):
        _, recv, _, devices, r = ring
        i = index(sense, h, k)
        remote(
            src, recv[sense].at[i], ring_send.at[r, sense], ring_recv.at[r, sense, i], devices[sense]
        ).start()

    def owner(ring, sense, k):
        return (ring[2] + (k if sense == 0 else 8 - k)) % 8

    def legs(k):
        for far in (0, 1):
            for p in (0, 1):
                yield 0, (2 * far + p), k - far
                yield 1, (2 - 2 * far + p), k - far

    def begin(ring):
        for sense, h, k in legs(4):
            hand(ring, sense, h, k, ring[0].at[owner(ring, sense, k), pl.ds(h * 4, 4)])

    def take(ring, sense, h, k):
        i = index(sense, h, k)
        arrived(ring[1][sense].at[i], ring_recv.at[ring[4], sense, i])
        return i

    def advance(ring, k):
        for sense, h, kk in legs(k):
            if kk < 2:
                continue
            i = take(ring, sense, h, kk)
            buf = ring[1][sense]
            mine = ring[0][owner(ring, sense, kk - 1), h * 4 : h * 4 + 4]
            buf[i] = (buf[i].astype(F32) + mine.astype(F32)).astype(BF)
            hand(ring, sense, h, kk - 1, buf.at[i])

    def close(ring, mid):
        for h in range(4):
            i = take(ring, 0, h, 1)
            j = take(ring, 1, h, 1)
            mine = ring[0][ring[2], h * 4 : h * 4 + 4]
            mid[h * 4 : h * 4 + 4] = (
                mine.astype(F32) + ring[1][0][i].astype(F32) + ring[1][1][j].astype(F32)
            ).astype(BF)

    def direct_z(o):
        g, device = group_xy(o)
        return remote(z_mid.at[g], z_in.at[gy], far_send.at[0], far_recv.at[0], device)

    def direct_y(o):
        g, device = group_xz(o)
        return remote(y_mid.at[g], y_in.at[gz], far_send.at[1], far_recv.at[1], device)

    def send_direct(direct):
        def step(o, carry):
            direct(o).start()
            return carry

        lax.fori_loop(1, 16, step, 0)

    for i in (1, 2, 3):
        if i > 1:
            hear(0, i)
            hear(1, i)
    apply_operator(0)
    product(0)
    begin(rings[0])
    hear(0, 5)
    tell(0, 7)
    hear(1, 5)
    tell(1, 7)
    advance(rings[0], 4)
    for i in (6, 7):
        hear(0, i)
        hear(1, i)
    apply_operator(1)
    product(1)
    begin(rings[1])
    advance(rings[0], 3)
    advance(rings[0], 2)
    advance(rings[1], 4)
    close(rings[0], z_mid)
    send_direct(direct_z)
    z_in[gy] = z_mid[gy]
    advance(rings[1], 3)
    advance(rings[1], 2)
    close(rings[1], y_mid)
    send_direct(direct_y)
    y_in[gz] = y_mid[gz]

    spot = lax.broadcasted_iota(jnp.int32, (16, 512), 0) + (me % 32) * 16
    on_tile = lax.broadcasted_iota(jnp.int32, (16, 512), 1) == spot

    def column(row):
        spread = jnp.where(on_tile, jnp.broadcast_to(row, (16, 512)), F32(0))
        return jnp.sum(spread, axis=1, keepdims=True)

    def frequency(block):
        at = midx_ref[block]
        high = lax.broadcasted_iota(jnp.int32, (384, 512), 0) == jnp.broadcast_to(at // 128, (384, 512))
        rows = lax.dot_general(
            spec_ref[...], high.astype(F32), (((0,), (0,)), ((), ())),
            precision=lax.Precision.HIGHEST, preferred_element_type=F32,
        )
        low = lax.broadcasted_iota(jnp.int32, (128, 512), 0) == jnp.broadcast_to(at % 128, (128, 512))
        return jnp.sum(jnp.where(low, rows, F32(0)), axis=0, keepdims=True)

    row_freq = frequency(mode)
    row_width = width_ref[mode]
    col_freq = column(frequency(me // 32))
    col_width = column(width_ref[me // 32])
    freq_sum = row_freq + col_freq
    spacing = row_freq - col_freq
    mean_width = 0.5 * (row_width + col_width)
    factor = freq_sum * freq_sum / (4.0 * row_freq * col_freq)
    weight = factor * mean_width / (spacing * spacing + mean_width * mean_width)

    fifteen = pl.ds(0, 15)
    arrived(z_in.at[fifteen], far_recv.at[0])
    arrived(y_in.at[fifteen], far_recv.at[1])
    tile = jnp.concatenate(
        [jnp.sum(z_in[...].astype(F32), axis=0), jnp.sum(y_in[...].astype(F32), axis=0)], axis=1
    )
    tile_ref[...] = tile
    share = jnp.sum(weight * tile * tile, axis=0, keepdims=True)

    for q in range(4):
        s_y[y, q : q + 1, :] = share[:, q * BS : (q + 1) * BS]
    for o in range(1, NY):
        remote(s_y.at[y], s_y.at[y], sum_send.at[0], sum_recv.at[0], at_y(o)).start()
    arrived(s_y.at[pl.ds(0, 7)], sum_recv.at[0])
    s_xz[gz] = jnp.sum(s_y[...], axis=0)
    for o in range(1, 16):
        remote(
            s_xz.at[gz], s_xz.at[gz], sum_send.at[1], sum_recv.at[1], group_xz(o)[1]
        ).start()
    arrived(s_xz.at[fifteen], sum_recv.at[1])
    diff_ref[...] = jnp.sum(s_xz[...], axis=0) * F32(1.0 / 2048)

    for copy in sends:
        copy.wait_send()

    for ref, sem in (
        (z_in.at[fifteen], far_send.at[0]), (y_in.at[fifteen], far_send.at[1]),
        (s_y.at[pl.ds(0, 7)], sum_send.at[0]), (s_xz.at[fifteen], sum_send.at[1]),
        (rz_plus, ring_send.at[0, 0]), (rz_minus, ring_send.at[0, 1]),
        (ry_plus, ring_send.at[1, 0]), (ry_minus, ring_send.at[1, 1]),
    ):
        remote(ref, ref, sem, sem, above).wait_send()


def body(eigvec, operator_blocks, column_blocks, block_mask, spectrum, mode_index, linewidth):
    anywhere = pl.BlockSpec(memory_space=pl.ANY)
    vmem = pl.BlockSpec(memory_space=pltpu.VMEM)
    dma = pltpu.SemaphoreType.DMA
    ring_buffer = pltpu.VMEM((14, 4, 16, 256), BF)
    tile, diff = pl.pallas_call(
        kernel,
        out_shape=(
            jax.ShapeDtypeStruct((16, 512), F32),
            jax.ShapeDtypeStruct((4, BS), F32),
        ),
        in_specs=[anywhere] * 7,
        out_specs=(vmem, vmem),
        scratch_shapes=[
            pltpu.VMEM((2, 11 * BS, 256), BF),
            pltpu.VMEM((3, LB * BS, 512), BF),
            pltpu.VMEM((4, 512, LB * BS), BF),
            pltpu.VMEM((LB, 8, BS, BS), BF),
            pltpu.SMEM((LB, 8), jnp.int32),
            pltpu.SMEM((LB, 8), jnp.int32),
            pltpu.VMEM((384, 128), F32),
            pltpu.VMEM((4, 1, 512), jnp.int32),
            pltpu.VMEM((4, 1, 512), F32),
            pltpu.VMEM((LB, BAND, BS, BS), BF),
            pltpu.VMEM((10, BS, BS), BF),
            pltpu.VMEM((10, BS, BS), BF),
            pltpu.VMEM((10, BS, BS), BF),
            pltpu.VMEM((10, BS, BS), BF),
            pltpu.VMEM((BS, BS), BF),
            pltpu.VMEM((BS, BS), BF),
            pltpu.VMEM((LB, BS, BAND * BS), BF),
            pltpu.VMEM((2, LB * BS, 256), BF),
            pltpu.VMEM((NZ, 16, 16, 256), BF),
            pltpu.VMEM((NY, 16, 16, 256), BF),
            ring_buffer, ring_buffer, ring_buffer, ring_buffer,
            pltpu.VMEM((16, 16, 256), BF),
            pltpu.VMEM((16, 16, 256), BF),
            pltpu.VMEM((16, 16, 256), BF),
            pltpu.VMEM((16, 16, 256), BF),
            pltpu.VMEM((NY, 4, BS), F32),
            pltpu.VMEM((16, 4, BS), F32),
            dma((8,)), dma((5,)), dma((5,)), dma((2,)), dma((2,)), dma((2, 8)), dma((2, 8)),
            dma((2, 2)), dma((2, 2, 14)), dma((2,)), dma((2,)), dma((2,)), dma((2,)),
        ],
        compiler_params=pltpu.CompilerParams(
            collective_id=0, has_side_effects=True, vmem_limit_bytes=40 * 1024 * 1024
        ),
    )(
        *(
            pltpu.with_memory_space_constraint(array, pltpu.HBM)
            for array in (
                eigvec, operator_blocks, column_blocks, block_mask,
                spectrum.reshape(384, 128), mode_index.reshape(4, 1, 512),
                linewidth.reshape(4, 1, 512),
            )
        )
    )
    return tile.T, diff.reshape(512)


def solution(mesh):
    in_specs = (
        P("atoms", "modes"),
        P("atoms", None, None, None),
        P("atoms", None),
        P("atoms", None),
        P(),
        P(),
        P(),
    )
    out_specs = (P("modes", "atoms"), P("modes"))
    return jax.shard_map(body, mesh=mesh, in_specs=in_specs, out_specs=out_specs, check_vma=False)
```

time: 87.2 us -> 78.3 us (0.90)
  the two profiles are of different devices: /device:TPU:2 before, /device:TPU:6 now
where the time goes in v2:
time: 78.3 us; the launch traced here: 78.1 us
  Pallas kernels  76.3 us (97%)
  local copies, waits for them, and re-layouts  1.2 us (2%)
    pallas_call x1, Pallas kernels, body(): pl.pallas_call(kernel, out_shape=(jax.ShapeDtypeStruct((16, 512), F32), j...  76.3 us

profile of v2, /device:TPU:6, one launch (start us, length us, event | category | flops | bytes accessed | tf_op | source)
XLA Modules:
  0.0 78.1 jit_solution(11951687949185457738)
XLA Ops:
  0.6 76.3 %shard_map.86 = (f32[16,512]{1,0:T(8,128)S(1)}, f32[4,128]{1,0:T(4,128)S(1)}) custom-call(bf16[384,512]{1,0:T(8,128)(2,1)} %e_hbm.1, bf16[3,8,128,128]{3,2,1,0:T(8,128)(2,1)} %op_hbm.1, s32[3,8]{1,0:T(4,128)} %col_hbm.1, s32[3,8]{1,0:T(4,128)} %mask_hbm.1, f32[384,128]{1,0:T(8,128)} %bitcast.7, s32[4,1,512]{2,1,0:T(1,128)} %bitcast.8, f32[4,1,512]{2,1,0:T(1,128)} %bitcast.9), custom_call_target="tpu_custom_call" | custom-call | tf_op jit(solution)/shard_map/pallas_call | solution.py:458
  76.9 0.6 copy.11
  77.5 0.6 copy.12

commit v3 on v2

--- a/solution.py
+++ b/solution.py
@@ -26,7 +26,7 @@
     dense, up_send, dn_send, lo_blk, hi_blk, lo_far, hi_far,
     bmat, wmat, pz, py, rz_plus, rz_minus, ry_plus, ry_minus, z_mid, y_mid, z_in, y_in,
     s_y, s_xz,
-    load_sem, mode_send, mode_recv, blk_send, blk_recv, msg_send, msg_recv,
+    load_sem, mode_send, mode_recv, blk_send, blk_recv, msg_send, msg_recv, past_send,
     ring_send, ring_recv, far_send, far_recv, sum_send, sum_recv,
 ):
     me = lax.axis_index("atoms")
@@ -60,6 +60,8 @@
 
     top = (y == NY - 1) & (z == NZ - 1)
     bottom = (y == 0) & (z == 0)
+    before_top = (y == NY - 2) & (z == NZ - 1)
+    before_bottom = (y == 1) & (z == 0)
     above_across = ((me + 1) % ATOMS, across_mode)
     below_across = ((me + ATOMS - 1) % ATOMS, across_mode)
 
@@ -103,6 +105,104 @@
         greet(below_across)
 
     extra = jnp.where(top | bottom, 1, 0)
+
+    pl.semaphore_wait(barrier, 36 + extra)
+
+    sends = []
+    guarded = []
+
+    def go(*args):
+        copy = remote(*args)
+        copy.start()
+        sends.append(copy)
+        return copy
+
+    def arrived(dst, sem):
+        remote(dst, dst, sem, sem, above).wait_recv()
+
+    half = pl.ds(core * 5, 5)
+    other_half = pl.ds((1 - core) * 5, 5)
+    messages = [[(up_send.at[half], lo_blk.at[half])], [(dn_send.at[half], hi_blk.at[half])]]
+    for h in range(2):
+        lanes = pl.ds(h * 256, 256)
+        rows = ext.at[h]
+        messages[0] += [
+            (e_hbm.at[pl.ds(256, 128), lanes], rows.at[pl.ds(384, 128)]),
+            (e_hbm.at[pl.ds(0, 256), lanes], rows.at[pl.ds(128, 256)]),
+            (rows.at[pl.ds(384, 128)], rows.at[pl.ds(0, 128)]),
+        ]
+        messages[1] += [
+            (e_hbm.at[pl.ds(0, 128), lanes], rows.at[pl.ds(896, 128)]),
+            (e_hbm.at[pl.ds(128, 256), lanes], rows.at[pl.ds(1024, 256)]),
+            (rows.at[pl.ds(896, 128)], rows.at[pl.ds(1280, 128)]),
+        ]
+        if h == 0:
+            messages[0].append((up_send.at[8], lo_far))
+            messages[1].append((dn_send.at[8], hi_far))
+
+    def message(way, i):
+        src, dst = messages[way][i]
+        atoms, edge = (above[0], top) if way == 0 else (below[0], bottom)
+        to_mode = jnp.where(edge, across_mode, mode) if i == 0 else mode
+        if i == 4:
+            atoms = (me + (2 if way == 0 else ATOMS - 2)) % ATOMS
+        return remote(src, dst, msg_send.at[way, i], msg_recv.at[way, i], (atoms, to_mode)), edge
+
+    def tell(way, i):
+        copy, edge = message(way, i)
+        if i in (0, 4):
+            copy.start()
+        else:
+            pl.when(jnp.logical_not(edge))(copy.start)
+
+    def tell_past_corner(way):
+        edge = before_top if way == 0 else before_bottom
+        atoms = (me + (2 if way == 0 else ATOMS - 2)) % ATOMS
+        for h in range(2):
+            copy = remote(
+                messages[way][4 * h + 1][0], messages[way][4 * h + 3][1],
+                past_send.at[h], msg_recv.at[way, 4 * h + 3], (atoms, mode),
+            )
+            pl.when(edge)(copy.start)
+            guarded.append((jnp.logical_not(edge), copy))
+
+    def tell_both(i):
+        tell(0, i)
+        tell(1, i)
+
+    near_rows = pl.ds(pl.multiple_of(jnp.where(bottom, 0, 2 * BS), BS), BS)
+    rest_rows = pl.ds(pl.multiple_of(jnp.where(bottom, BS, 0), BS), 2 * BS)
+    pieces = (
+        (near_rows, pl.ds(0, 512)), (rest_rows, pl.ds(0, 256)), (rest_rows, pl.ds(256, 256))
+    )
+
+    def piece(n, p):
+        return others.at[n, pieces[p][0], pieces[p][1]]
+
+    def relay(p):
+        for way, edge, device in ((0, top, above_across), (1, bottom, below_across)):
+
+            @pl.when(edge)
+            def _():
+                for h in range(2):
+                    if p not in (0, h + 1):
+                        continue
+                    i = 4 * h + (1 if p == 0 else 2)
+                    src = others.at[0, pieces[p][0], pl.ds(h * 256, 256)]
+                    remote(
+                        src, messages[way][i][1], msg_send.at[way, i], msg_recv.at[way, i], device
+                    ).start()
+
+    def hear(way, i):
+        arrived(messages[way][i][1], msg_recv.at[way, i])
+
+    for p in range(3):
+        go(e_hbm.at[pieces[p][0], pieces[p][1]], piece(0, p), mode_send.at[p], mode_recv.at[p], across)
+    go(e_hbm, others.at[1], mode_send.at[3], mode_recv.at[3], twin)
+    for way in (0, 1):
+        tell_past_corner(way)
+    tell_both(1)
+    tell_both(5)
 
     for copy in loads[:3]:
         copy.wait()
@@ -125,91 +225,12 @@
     up_send[9] = jnp.zeros((BS, BS), BF)
     dn_send[9] = jnp.zeros((BS, BS), BF)
 
-    pl.semaphore_wait(barrier, 36 + extra)
-
-    sends = []
-
-    def go(*args):
-        copy = remote(*args)
-        copy.start()
-        sends.append(copy)
-        return copy
-
-    def arrived(dst, sem):
-        remote(dst, dst, sem, sem, above).wait_recv()
-
-    half = pl.ds(core * 5, 5)
-    other_half = pl.ds((1 - core) * 5, 5)
-    messages = [[(up_send.at[half], lo_blk.at[half])], [(dn_send.at[half], hi_blk.at[half])]]
-    for h in range(2):
-        lanes = pl.ds(h * 256, 256)
-        rows = ext.at[h]
-        messages[0] += [
-            (e_hbm.at[pl.ds(256, 128), lanes], rows.at[pl.ds(384, 128)]),
-            (e_hbm.at[pl.ds(0, 256), lanes], rows.at[pl.ds(128, 256)]),
-            (rows.at[pl.ds(384, 128)], rows.at[pl.ds(0, 128)]),
-        ]
-        messages[1] += [
-            (e_hbm.at[pl.ds(0, 128), lanes], rows.at[pl.ds(896, 128)]),
-            (e_hbm.at[pl.ds(128, 256), lanes], rows.at[pl.ds(1024, 256)]),
-            (rows.at[pl.ds(896, 128)], rows.at[pl.ds(1280, 128)]),
-        ]
-        if h == 0:
-            messages[0].append((up_send.at[8], lo_far))
-            messages[1].append((dn_send.at[8], hi_far))
-
-    def tell(way, i):
-        src, dst = messages[way][i]
-        atoms, edge = (above[0], top) if way == 0 else (below[0], bottom)
-        to_mode = jnp.where(edge, across_mode, mode) if i == 0 else mode
-        if i == 4:
-            atoms = (me + (2 if way == 0 else ATOMS - 2)) % ATOMS
-        copy = remote(src, dst, msg_send.at[way, i], msg_recv.at[way, i], (atoms, to_mode))
-        sends.append(copy)
-        if i in (1, 2, 5, 6):
-            pl.when(jnp.logical_not(edge))(copy.start)
-        else:
-            copy.start()
-
-    def tell_both(i):
-        tell(0, i)
-        tell(1, i)
-
-    def tell_for_across(way, i):
-        h = i // 4
-        start, count = (((256, 128), (0, 256)) if way == 0 else ((0, 128), (128, 256)))[i % 4 - 1]
-        src = others.at[0, pl.ds(start, count), pl.ds(h * 256, 256)]
-        remote(
-            src, messages[way][i][1], msg_send.at[way, i], msg_recv.at[way, i],
-            (above_across, below_across)[way],
-        ).start()
-
-    def lanes_of(h):
-        return others.at[0, :, pl.ds(h * 256, 256)]
-
-    def gather_arrived(h):
-        arrived(lanes_of(h), mode_recv.at[h])
-
-    def relay(h):
-        for way, edge in ((0, top), (1, bottom)):
-
-            @pl.when(edge)
-            def _():
-                gather_arrived(h)
-                tell_for_across(way, 4 * h + 1)
-                tell_for_across(way, 4 * h + 2)
-
-    def hear(way, i):
-        arrived(messages[way][i][1], msg_recv.at[way, i])
-
-    for h in range(2):
-        go(e_hbm.at[:, pl.ds(h * 256, 256)], lanes_of(h), mode_send.at[h], mode_recv.at[h], across)
-    go(e_hbm, others.at[1], mode_send.at[2], mode_recv.at[2], twin)
-    for i in (0, 1, 2, 4, 5):
-        tell_both(i)
-
-    def turn(slot_mode, b, block):
-        turned[slot_mode, :, b * BS : (b + 1) * BS] = block.T
+    tell_both(0)
+    tell_both(2)
+    tell_both(4)
+    corner = top | bottom
+    not_corner = jnp.logical_not(corner)
+    pl.when(corner)(functools.partial(tell_both, 6))
 
     def build(r, d, mirror):
         value = mirror.astype(F32).T - dense[r, d].astype(F32)
@@ -227,17 +248,41 @@
                 h, (REACH + b) * BS : (REACH + b + 1) * BS
             ].T
 
-    relay(0)
+    def turn_other(n, slot_mode, p):
+        for b in range(LB):
+            turned[slot_mode, p * BS : (p + 1) * BS, b * BS : (b + 1) * BS] = others[
+                n, b * BS : (b + 1) * BS, p * BS : (p + 1) * BS
+            ].T
+
+    def hand_over(p):
+        arrived(piece(0, p), mode_recv.at[p])
+        relay(p)
+        go(piece(0, p), piece(2, p), mode_send.at[4 + p], mode_recv.at[4 + p], twin)
+
+    def pass_far(h):
+        for way in (0, 1):
+            hear(way, 4 * h + 1)
+            tell(way, 4 * h + 3)
+
+    def pass_both():
+        pass_far(0)
+        pass_far(1)
+
+    @pl.when(not_corner)
+    def _():
+        pass_both()
+        tell_both(6)
+
+    hand_over(0)
+    hand_over(1)
     hear(0, 0)
     go(lo_blk.at[half], lo_blk.at[half], blk_send.at[0], blk_recv.at[0], twin)
     hear(1, 0)
     go(hi_blk.at[half], hi_blk.at[half], blk_send.at[1], blk_recv.at[1], twin)
-    hear(0, 1)
-    tell(0, 3)
-    hear(1, 1)
-    tell(1, 3)
-    tell_both(6)
-    relay(1)
+    hand_over(2)
+    pl.when(corner)(pass_both)
+    for p in range(4):
+        turn_other(0, across_mode, p)
 
     arrived(lo_blk.at[other_half], blk_recv.at[0])
     arrived(hi_blk.at[other_half], blk_recv.at[1])
@@ -249,23 +294,13 @@
         r = d + c - 1
         build(r, c + 7 - r, hi_blk[k])
 
-    arrived(others.at[1], mode_recv.at[2])
-    for b in range(LB):
-        turn(twin_mode, b, others[1, b * BS : (b + 1) * BS, :])
-    for h in range(2):
-        pl.when(jnp.logical_not(top | bottom))(functools.partial(gather_arrived, h))
-        half_lanes = pl.ds(h * 256, 256)
-        go(lanes_of(h), others.at[2, :, half_lanes], mode_send.at[3 + h], mode_recv.at[3 + h], twin)
-        for b in range(LB):
-            turned[across_mode, h * 256 : (h + 1) * 256, b * BS : (b + 1) * BS] = others[
-                0, b * BS : (b + 1) * BS, h * 256 : (h + 1) * 256
-            ].T
-    for h in range(2):
-        arrived(others.at[2, :, pl.ds(h * 256, 256)], mode_recv.at[3 + h])
-        for b in range(LB):
-            turned[last_mode, h * 256 : (h + 1) * 256, b * BS : (b + 1) * BS] = others[
-                2, b * BS : (b + 1) * BS, h * 256 : (h + 1) * 256
-            ].T
+    arrived(others.at[1], mode_recv.at[3])
+    for p in range(4):
+        turn_other(1, twin_mode, p)
+    for p in range(3):
+        arrived(piece(2, p), mode_recv.at[4 + p])
+    for p in range(4):
+        turn_other(2, last_mode, p)
 
     hear(0, 4)
     build(0, 0, lo_far[...])
@@ -289,60 +324,62 @@
                     py[:, mb * 4 + q] = rows
             return carry
 
-        lax.fori_loop(0, 4, step, 0)
-
-    def index(sense, h, k):
-        long = h // 2 == sense
-        return (4 - k if long else 7 - k) * 2 + h % 2
+        for mb in range(4):
+            step(mb, 0)
 
     rings = (
-        (pz, (rz_plus, rz_minus), z, (at_z(1), at_z(NZ - 1)), 0),
-        (py, (ry_plus, ry_minus), y, (at_y(1), at_y(NY - 1)), 1),
+        (pz, (rz_plus, rz_minus), z, at_z, 0),
+        (py, (ry_plus, ry_minus), y, at_y, 1),
     )
-
-    def hand(ring, sense, h, k, src):
-        _, recv, _, devices, r = ring
-        i = index(sense, h, k)
-        remote(
-            src, recv[sense].at[i], ring_send.at[r, sense], ring_recv.at[r, sense, i], devices[sense]
-        ).start()
 
     def owner(ring, sense, k):
         return (ring[2] + (k if sense == 0 else 8 - k)) % 8
 
-    def legs(k):
-        for far in (0, 1):
-            for p in (0, 1):
-                yield 0, (2 * far + p), k - far
-                yield 1, (2 - 2 * far + p), k - far
+    def hand(ring, sense, i, steps, src):
+        device = ring[3](steps if sense == 0 else 8 - steps)
+        r = ring[4]
+        remote(
+            src, ring[1][sense].at[i], ring_send.at[r, sense], ring_recv.at[r, sense, i], device
+        ).start()
+
+    def slot(h, k):
+        return 2 + (3 - k) * 4 + h
+
+    def quarters():
+        for n in range(4):
+            yield 0, (n + 2) % 4
+            yield 1, n
 
     def begin(ring):
-        for sense, h, k in legs(4):
-            hand(ring, sense, h, k, ring[0].at[owner(ring, sense, k), pl.ds(h * 4, 4)])
-
-    def take(ring, sense, h, k):
-        i = index(sense, h, k)
-        arrived(ring[1][sense].at[i], ring_recv.at[ring[4], sense, i])
-        return i
+        for p in range(2):
+            for sense in range(2):
+                src = ring[0].at[owner(ring, sense, 4), pl.ds((2 * sense + p) * 4, 4)]
+                hand(ring, sense, p, 2, src)
+        for sense, h in quarters():
+            src = ring[0].at[owner(ring, sense, 3), pl.ds(h * 4, 4)]
+            hand(ring, sense, slot(h, 3), 1, src)
+
+    def take(ring, sense, i):
+        buf = ring[1][sense]
+        arrived(buf.at[i], ring_recv.at[ring[4], sense, i])
+        return buf[i].astype(F32)
 
     def advance(ring, k):
-        for sense, h, kk in legs(k):
-            if kk < 2:
-                continue
-            i = take(ring, sense, h, kk)
+        for sense, h in quarters():
+            i = slot(h, k)
+            mine = ring[0][owner(ring, sense, k - 1), h * 4 : h * 4 + 4]
+            total = take(ring, sense, i) + mine.astype(F32)
+            if k == 3 and h // 2 == sense:
+                total = total + take(ring, sense, h % 2)
             buf = ring[1][sense]
-            mine = ring[0][owner(ring, sense, kk - 1), h * 4 : h * 4 + 4]
-            buf[i] = (buf[i].astype(F32) + mine.astype(F32)).astype(BF)
-            hand(ring, sense, h, kk - 1, buf.at[i])
+            buf[i] = total.astype(BF)
+            hand(ring, sense, slot(h, k - 1), 1, buf.at[i])
 
     def close(ring, mid):
         for h in range(4):
-            i = take(ring, 0, h, 1)
-            j = take(ring, 1, h, 1)
-            mine = ring[0][ring[2], h * 4 : h * 4 + 4]
-            mid[h * 4 : h * 4 + 4] = (
-                mine.astype(F32) + ring[1][0][i].astype(F32) + ring[1][1][j].astype(F32)
-            ).astype(BF)
+            mine = ring[0][ring[2], h * 4 : h * 4 + 4].astype(F32)
+            both = take(ring, 0, slot(h, 1)) + take(ring, 1, slot(h, 1))
+            mid[h * 4 : h * 4 + 4] = (mine + both).astype(BF)
 
     def direct_z(o):
         g, device = group_xy(o)
@@ -359,34 +396,22 @@
 
         lax.fori_loop(1, 16, step, 0)
 
-    for i in (1, 2, 3):
-        if i > 1:
-            hear(0, i)
-            hear(1, i)
-    apply_operator(0)
-    product(0)
-    begin(rings[0])
-    hear(0, 5)
-    tell(0, 7)
-    hear(1, 5)
-    tell(1, 7)
-    advance(rings[0], 4)
-    for i in (6, 7):
-        hear(0, i)
-        hear(1, i)
-    apply_operator(1)
-    product(1)
-    begin(rings[1])
+    for h in range(2):
+        for way in (0, 1):
+            hear(way, 4 * h + 2)
+            hear(way, 4 * h + 3)
+        apply_operator(h)
+        product(h)
+        begin(rings[h])
     advance(rings[0], 3)
+    advance(rings[1], 3)
     advance(rings[0], 2)
-    advance(rings[1], 4)
+    advance(rings[1], 2)
     close(rings[0], z_mid)
     send_direct(direct_z)
-    z_in[gy] = z_mid[gy]
-    advance(rings[1], 3)
-    advance(rings[1], 2)
     close(rings[1], y_mid)
     send_direct(direct_y)
+    z_in[gy] = z_mid[gy]
     y_in[gz] = y_mid[gz]
 
     spot = lax.broadcasted_iota(jnp.int32, (16, 512), 0) + (me % 32) * 16
@@ -438,8 +463,17 @@
     arrived(s_xz.at[fifteen], sum_recv.at[1])
     diff_ref[...] = jnp.sum(s_xz[...], axis=0) * F32(1.0 / 2048)
 
+    for way in (0, 1):
+        for i in range(8):
+            copy, edge = message(way, i)
+            if i in (3, 7):
+                guarded.append((edge, copy))
+            else:
+                sends.append(copy)
     for copy in sends:
         copy.wait_send()
+    for skipped, copy in guarded:
+        pl.when(jnp.logical_not(skipped))(copy.wait_send)
 
     for ref, sem in (
         (z_in.at[fifteen], far_send.at[0]), (y_in.at[fifteen], far_send.at[1]),
@@ -491,7 +525,7 @@
             pltpu.VMEM((16, 16, 256), BF),
             pltpu.VMEM((NY, 4, BS), F32),
             pltpu.VMEM((16, 4, BS), F32),
-            dma((8,)), dma((5,)), dma((5,)), dma((2,)), dma((2,)), dma((2, 8)), dma((2, 8)),
+            dma((8,)), dma((7,)), dma((7,)), dma((2,)), dma((2,)), dma((2, 8)), dma((2, 8)), dma((2,)),
             dma((2, 2)), dma((2, 2, 14)), dma((2,)), dma((2,)), dma((2,)), dma((2,)),
         ],
         compiler_params=pltpu.CompilerParams(

time: 78.3 us -> 72.4 us (0.925)
  the two profiles are of different devices: /device:TPU:6 before, /device:TPU:8 now
where the time goes in v3:
time: 72.4 us; the launch traced here: 72.3 us
  Pallas kernels  70.5 us (97%)
  local copies, waits for them, and re-layouts  1.2 us (2%)
    pallas_call x1, Pallas kernels, body(): pl.pallas_call(kernel, out_shape=(jax.ShapeDtypeStruct((16, 512), F32), j...  70.5 us

profile of v3, /device:TPU:8, one launch (start us, length us, event | category | flops | bytes accessed | tf_op | source)
XLA Modules:
  0.0 72.3 jit_solution(17750833022916483528)
XLA Ops:
  0.6 70.5 %shard_map.86 = (f32[16,512]{1,0:T(8,128)S(1)}, f32[4,128]{1,0:T(4,128)S(1)}) custom-call(bf16[384,512]{1,0:T(8,128)(2,1)} %e_hbm.1, bf16[3,8,128,128]{3,2,1,0:T(8,128)(2,1)} %op_hbm.1, s32[3,8]{1,0:T(4,128)} %col_hbm.1, s32[3,8]{1,0:T(4,128)} %mask_hbm.1, f32[384,128]{1,0:T(8,128)} %bitcast.7, s32[4,1,512]{2,1,0:T(1,128)} %bitcast.8, f32[4,1,512]{2,1,0:T(1,128)} %bitcast.9), custom_call_target="tpu_custom_call" | custom-call | tf_op jit(solution)/shard_map/pallas_call | solution.py:492
  71.1 0.6 copy.11
  71.7 0.6 copy.12

commit v4 on v3

--- a/solution.py
+++ b/solution.py
@@ -23,7 +23,7 @@
     e_hbm, op_hbm, col_hbm, mask_hbm, spec_hbm, midx_hbm, width_hbm,
     tile_ref, diff_ref,
     ext, others, turned, opv, col_s, mask_s, spec_ref, midx_ref, width_ref,
-    dense, up_send, dn_send, lo_blk, hi_blk, lo_far, hi_far,
+    dense, up_send, dn_send, lo_blk, hi_blk, far_out, far_in,
     bmat, wmat, pz, py, rz_plus, rz_minus, ry_plus, ry_minus, z_mid, y_mid, z_in, y_in,
     s_y, s_xz,
     load_sem, mode_send, mode_recv, blk_send, blk_recv, msg_send, msg_recv, past_send,
@@ -64,6 +64,8 @@
     before_bottom = (y == 1) & (z == 0)
     above_across = ((me + 1) % ATOMS, across_mode)
     below_across = ((me + ATOMS - 1) % ATOMS, across_mode)
+    up_two_across = ((me + 2) % ATOMS, across_mode)
+    down_two_across = ((me + ATOMS - 2) % ATOMS, across_mode)
 
     def remote(src, dst, ssem, rsem, device):
         return pltpu.make_async_remote_copy(
@@ -99,12 +101,17 @@
     @pl.when(top)
     def _():
         greet(above_across)
+        greet(up_two_across)
 
     @pl.when(bottom)
     def _():
         greet(below_across)
-
-    extra = jnp.where(top | bottom, 1, 0)
+        greet(down_two_across)
+
+    pl.when(before_top)(functools.partial(greet, up_two_across))
+    pl.when(before_bottom)(functools.partial(greet, down_two_across))
+
+    extra = jnp.where(top | bottom, 2, 0) + jnp.where(before_top | before_bottom, 1, 0)
 
     pl.semaphore_wait(barrier, 36 + extra)
 
@@ -120,8 +127,8 @@
     def arrived(dst, sem):
         remote(dst, dst, sem, sem, above).wait_recv()
 
-    half = pl.ds(core * 5, 5)
-    other_half = pl.ds((1 - core) * 5, 5)
+    half = pl.ds(core * 4, 4)
+    other_half = pl.ds((1 - core) * 4, 4)
     messages = [[(up_send.at[half], lo_blk.at[half])], [(dn_send.at[half], hi_blk.at[half])]]
     for h in range(2):
         lanes = pl.ds(h * 256, 256)
@@ -137,43 +144,42 @@
             (rows.at[pl.ds(896, 128)], rows.at[pl.ds(1280, 128)]),
         ]
         if h == 0:
-            messages[0].append((up_send.at[8], lo_far))
-            messages[1].append((dn_send.at[8], hi_far))
+            messages[0].append(None)
+            messages[1].append(None)
 
     def message(way, i):
         src, dst = messages[way][i]
         atoms, edge = (above[0], top) if way == 0 else (below[0], bottom)
         to_mode = jnp.where(edge, across_mode, mode) if i == 0 else mode
-        if i == 4:
-            atoms = (me + (2 if way == 0 else ATOMS - 2)) % ATOMS
         return remote(src, dst, msg_send.at[way, i], msg_recv.at[way, i], (atoms, to_mode)), edge
 
     def tell(way, i):
         copy, edge = message(way, i)
-        if i in (0, 4):
+        if i == 0:
             copy.start()
         else:
             pl.when(jnp.logical_not(edge))(copy.start)
 
-    def tell_past_corner(way):
-        edge = before_top if way == 0 else before_bottom
-        atoms = (me + (2 if way == 0 else ATOMS - 2)) % ATOMS
-        for h in range(2):
-            copy = remote(
-                messages[way][4 * h + 1][0], messages[way][4 * h + 3][1],
-                past_send.at[h], msg_recv.at[way, 4 * h + 3], (atoms, mode),
-            )
-            pl.when(edge)(copy.start)
-            guarded.append((jnp.logical_not(edge), copy))
+    def past_corner(way, h):
+        rows = pl.ds(2 * BS, BS) if way == 0 else pl.ds(0, BS)
+        return remote(
+            others.at[0, rows, pl.ds(h * 256, 256)], messages[way][4 * h + 3][1],
+            past_send.at[h], msg_recv.at[way, 4 * h + 3], (up_two_across, down_two_across)[way],
+        )
+
+    def tell_past_corner(h):
+        for way, edge in ((0, before_top), (1, before_bottom)):
+            pl.when(edge)(past_corner(way, h).start)
 
     def tell_both(i):
         tell(0, i)
         tell(1, i)
 
-    near_rows = pl.ds(pl.multiple_of(jnp.where(bottom, 0, 2 * BS), BS), BS)
-    rest_rows = pl.ds(pl.multiple_of(jnp.where(bottom, BS, 0), BS), 2 * BS)
+    near_rows = pl.ds(pl.multiple_of(jnp.where(bottom | before_bottom, 0, 2 * BS), BS), BS)
+    rest_rows = pl.ds(pl.multiple_of(jnp.where(bottom | before_bottom, BS, 0), BS), 2 * BS)
     pieces = (
-        (near_rows, pl.ds(0, 512)), (rest_rows, pl.ds(0, 256)), (rest_rows, pl.ds(256, 256))
+        (near_rows, pl.ds(0, 256)), (near_rows, pl.ds(256, 256)),
+        (rest_rows, pl.ds(0, 256)), (rest_rows, pl.ds(256, 256)),
     )
 
     def piece(n, p):
@@ -184,23 +190,18 @@
 
             @pl.when(edge)
             def _():
-                for h in range(2):
-                    if p not in (0, h + 1):
-                        continue
-                    i = 4 * h + (1 if p == 0 else 2)
-                    src = others.at[0, pieces[p][0], pl.ds(h * 256, 256)]
-                    remote(
-                        src, messages[way][i][1], msg_send.at[way, i], msg_recv.at[way, i], device
-                    ).start()
+                i = (1, 5, 2, 6)[p]
+                remote(
+                    piece(0, p), messages[way][i][1],
+                    msg_send.at[way, i], msg_recv.at[way, i], device,
+                ).start()
 
     def hear(way, i):
         arrived(messages[way][i][1], msg_recv.at[way, i])
 
-    for p in range(3):
+    for p in range(4):
         go(e_hbm.at[pieces[p][0], pieces[p][1]], piece(0, p), mode_send.at[p], mode_recv.at[p], across)
-    go(e_hbm, others.at[1], mode_send.at[3], mode_recv.at[3], twin)
-    for way in (0, 1):
-        tell_past_corner(way)
+    go(e_hbm, others.at[1], mode_send.at[4], mode_recv.at[4], twin)
     tell_both(1)
     tell_both(5)
 
@@ -218,16 +219,16 @@
             keep = jnp.where(used > 0, F32(1), F32(0)).astype(F32)
             block = (opv[r, slot].astype(F32) * keep).astype(BF)
             dense[r, d] = block
-            if (r, d) in UP:
-                up_send[UP.index((r, d))] = block
-            if (r, d) in DOWN:
-                dn_send[DOWN.index((r, d))] = block
-    up_send[9] = jnp.zeros((BS, BS), BF)
-    dn_send[9] = jnp.zeros((BS, BS), BF)
+            for n, (table, send) in enumerate(((UP, up_send), (DOWN, dn_send))):
+                if (r, d) == table[8]:
+                    far_out[n] = block
+                elif (r, d) in table:
+                    send[table.index((r, d))] = block
 
     tell_both(0)
+    two_away = ((me + 2 - 4 * core + ATOMS) % ATOMS, mode)
+    go(far_out.at[core], far_in.at[core], blk_send.at[2], blk_recv.at[2], two_away)
     tell_both(2)
-    tell_both(4)
     corner = top | bottom
     not_corner = jnp.logical_not(corner)
     pl.when(corner)(functools.partial(tell_both, 6))
@@ -257,7 +258,7 @@
     def hand_over(p):
         arrived(piece(0, p), mode_recv.at[p])
         relay(p)
-        go(piece(0, p), piece(2, p), mode_send.at[4 + p], mode_recv.at[4 + p], twin)
+        go(piece(0, p), piece(2, p), mode_send.at[5 + p], mode_recv.at[5 + p], twin)
 
     def pass_far(h):
         for way in (0, 1):
@@ -268,19 +269,24 @@
         pass_far(0)
         pass_far(1)
 
+    for h in range(2):
+        hand_over(h)
+        tell_past_corner(h)
+
     @pl.when(not_corner)
     def _():
         pass_both()
         tell_both(6)
 
-    hand_over(0)
-    hand_over(1)
+    hand_over(2)
     hear(0, 0)
     go(lo_blk.at[half], lo_blk.at[half], blk_send.at[0], blk_recv.at[0], twin)
     hear(1, 0)
     go(hi_blk.at[half], hi_blk.at[half], blk_send.at[1], blk_recv.at[1], twin)
-    hand_over(2)
+    hand_over(3)
     pl.when(corner)(pass_both)
+    arrived(far_in.at[core], blk_recv.at[2])
+    go(far_in.at[core], far_in.at[core], blk_send.at[3], blk_recv.at[3], twin)
     for p in range(4):
         turn_other(0, across_mode, p)
 
@@ -294,18 +300,17 @@
         r = d + c - 1
         build(r, c + 7 - r, hi_blk[k])
 
-    arrived(others.at[1], mode_recv.at[3])
+    arrived(others.at[1], mode_recv.at[4])
     for p in range(4):
         turn_other(1, twin_mode, p)
-    for p in range(3):
-        arrived(piece(2, p), mode_recv.at[4 + p])
+    for p in range(4):
+        arrived(piece(2, p), mode_recv.at[5 + p])
     for p in range(4):
         turn_other(2, last_mode, p)
 
-    hear(0, 4)
-    build(0, 0, lo_far[...])
-    hear(1, 4)
-    build(2, 8, hi_far[...])
+    arrived(far_in.at[1 - core], blk_recv.at[3])
+    build(0, 0, far_in[0])
+    build(2, 8, far_in[1])
 
     def apply_operator(h):
         for r in range(LB):
@@ -362,23 +367,26 @@
     def take(ring, sense, i):
         buf = ring[1][sense]
         arrived(buf.at[i], ring_recv.at[ring[4], sense, i])
-        return buf[i].astype(F32)
+        return buf[i]
 
     def advance(ring, k):
         for sense, h in quarters():
             i = slot(h, k)
             mine = ring[0][owner(ring, sense, k - 1), h * 4 : h * 4 + 4]
-            total = take(ring, sense, i) + mine.astype(F32)
+            buf = ring[1][sense]
             if k == 3 and h // 2 == sense:
-                total = total + take(ring, sense, h % 2)
-            buf = ring[1][sense]
-            buf[i] = total.astype(BF)
+                buf[i] = (
+                    take(ring, sense, i).astype(F32) + mine.astype(F32)
+                    + take(ring, sense, h % 2).astype(F32)
+                ).astype(BF)
+            else:
+                buf[i] = take(ring, sense, i) + mine
             hand(ring, sense, slot(h, k - 1), 1, buf.at[i])
 
     def close(ring, mid):
         for h in range(4):
             mine = ring[0][ring[2], h * 4 : h * 4 + 4].astype(F32)
-            both = take(ring, 0, slot(h, 1)) + take(ring, 1, slot(h, 1))
+            both = take(ring, 0, slot(h, 1)).astype(F32) + take(ring, 1, slot(h, 1)).astype(F32)
             mid[h * 4 : h * 4 + 4] = (mine + both).astype(BF)
 
     def direct_z(o):
@@ -396,13 +404,20 @@
 
         lax.fori_loop(1, 16, step, 0)
 
-    for h in range(2):
-        for way in (0, 1):
-            hear(way, 4 * h + 2)
-            hear(way, 4 * h + 3)
-        apply_operator(h)
-        product(h)
-        begin(rings[h])
+    hear(0, 2)
+    hear(1, 2)
+    hear(0, 3)
+    hear(1, 3)
+    apply_operator(0)
+    product(0)
+    begin(rings[0])
+    hear(0, 6)
+    hear(1, 6)
+    hear(0, 7)
+    hear(1, 7)
+    apply_operator(1)
+    product(1)
+    begin(rings[1])
     advance(rings[0], 3)
     advance(rings[1], 3)
     advance(rings[0], 2)
@@ -464,12 +479,15 @@
     diff_ref[...] = jnp.sum(s_xz[...], axis=0) * F32(1.0 / 2048)
 
     for way in (0, 1):
-        for i in range(8):
+        for i in (0, 1, 2, 3, 5, 6, 7):
             copy, edge = message(way, i)
             if i in (3, 7):
                 guarded.append((edge, copy))
             else:
                 sends.append(copy)
+        for h in range(2):
+            edge = (before_top, before_bottom)[way]
+            guarded.append((jnp.logical_not(edge), past_corner(way, h)))
     for copy in sends:
         copy.wait_send()
     for skipped, copy in guarded:
@@ -508,12 +526,12 @@
             pltpu.VMEM((4, 1, 512), jnp.int32),
             pltpu.VMEM((4, 1, 512), F32),
             pltpu.VMEM((LB, BAND, BS, BS), BF),
-            pltpu.VMEM((10, BS, BS), BF),
-            pltpu.VMEM((10, BS, BS), BF),
-            pltpu.VMEM((10, BS, BS), BF),
-            pltpu.VMEM((10, BS, BS), BF),
-            pltpu.VMEM((BS, BS), BF),
-            pltpu.VMEM((BS, BS), BF),
+            pltpu.VMEM((8, BS, BS), BF),
+            pltpu.VMEM((8, BS, BS), BF),
+            pltpu.VMEM((8, BS, BS), BF),
+            pltpu.VMEM((8, BS, BS), BF),
+            pltpu.VMEM((2, BS, BS), BF),
+            pltpu.VMEM((2, BS, BS), BF),
             pltpu.VMEM((LB, BS, BAND * BS), BF),
             pltpu.VMEM((2, LB * BS, 256), BF),
             pltpu.VMEM((NZ, 16, 16, 256), BF),
@@ -525,7 +543,7 @@
             pltpu.VMEM((16, 16, 256), BF),
             pltpu.VMEM((NY, 4, BS), F32),
             pltpu.VMEM((16, 4, BS), F32),
-            dma((8,)), dma((7,)), dma((7,)), dma((2,)), dma((2,)), dma((2, 8)), dma((2, 8)), dma((2,)),
+            dma((8,)), dma((9,)), dma((9,)), dma((4,)), dma((4,)), dma((2, 8)), dma((2, 8)), dma((2,)),
             dma((2, 2)), dma((2, 2, 14)), dma((2,)), dma((2,)), dma((2,)), dma((2,)),
         ],
         compiler_params=pltpu.CompilerParams(

time: 72.4 us -> 71.4 us (0.986)
  Pallas kernels: 70.5 us -> 69.4 us
    pallas_call x1, Pallas kernels: 70.5 us -> 69.4 us  [body(): pl.pallas_call(kernel, out_shape=(jax.ShapeDtypeStruct((16, 512), F32), j...]
where the time goes in v4:
time: 71.4 us; the launch traced here: 71.3 us
  Pallas kernels  69.4 us (97%)
  local copies, waits for them, and re-layouts  1.2 us (2%)
    pallas_call x1, Pallas kernels, body(): pl.pallas_call(kernel, out_shape=(jax.ShapeDtypeStruct((16, 512), F32), j...  69.4 us

profile of v4, /device:TPU:8, one launch (start us, length us, event | category | flops | bytes accessed | tf_op | source)
XLA Modules:
  0.0 71.3 jit_solution(13290891112232812687)
XLA Ops:
  0.6 69.4 %shard_map.86 = (f32[16,512]{1,0:T(8,128)S(1)}, f32[4,128]{1,0:T(4,128)S(1)}) custom-call(bf16[384,512]{1,0:T(8,128)(2,1)} %e_hbm.1, bf16[3,8,128,128]{3,2,1,0:T(8,128)(2,1)} %op_hbm.1, s32[3,8]{1,0:T(4,128)} %col_hbm.1, s32[3,8]{1,0:T(4,128)} %mask_hbm.1, f32[384,128]{1,0:T(8,128)} %bitcast.7, s32[4,1,512]{2,1,0:T(1,128)} %bitcast.8, f32[4,1,512]{2,1,0:T(1,128)} %bitcast.9), custom_call_target="tpu_custom_call" | custom-call | tf_op jit(solution)/shard_map/pallas_call | solution.py:510
  70.1 0.6 copy.11
  70.7 0.6 copy.12

commit v5 on v4

--- a/solution.py
+++ b/solution.py
@@ -356,13 +356,15 @@
             yield 1, n
 
     def begin(ring):
-        for p in range(2):
-            for sense in range(2):
-                src = ring[0].at[owner(ring, sense, 4), pl.ds((2 * sense + p) * 4, 4)]
-                hand(ring, sense, p, 2, src)
-        for sense, h in quarters():
+        for n, (sense, h) in enumerate(quarters()):
             src = ring[0].at[owner(ring, sense, 3), pl.ds(h * 4, 4)]
             hand(ring, sense, slot(h, 3), 1, src)
+            if n != 3:
+                continue
+            for p in range(2):
+                for way in range(2):
+                    far = ring[0].at[owner(ring, way, 4), pl.ds((2 * way + p) * 4, 4)]
+                    hand(ring, way, p, 2, far)
 
     def take(ring, sense, i):
         buf = ring[1][sense]

time: 71.4 us -> 70.4 us (0.986)
  Pallas kernels: 69.4 us -> 68.5 us
    pallas_call x1, Pallas kernels: 69.4 us -> 68.5 us  [body(): pl.pallas_call(kernel, out_shape=(jax.ShapeDtypeStruct((16, 512), F32), j...]
where the time goes in v5:
time: 70.4 us; the launch traced here: 70.3 us
  Pallas kernels  68.5 us (97%)
  local copies, waits for them, and re-layouts  1.2 us (2%)
    pallas_call x1, Pallas kernels, body(): pl.pallas_call(kernel, out_shape=(jax.ShapeDtypeStruct((16, 512), F32), j...  68.5 us

profile of v5, /device:TPU:8, one launch (start us, length us, event | category | flops | bytes accessed | tf_op | source)
XLA Modules:
  0.0 70.3 jit_solution(9725118248669087207)
XLA Ops:
  0.6 68.5 %shard_map.86 = (f32[16,512]{1,0:T(8,128)S(1)}, f32[4,128]{1,0:T(4,128)S(1)}) custom-call(bf16[384,512]{1,0:T(8,128)(2,1)} %e_hbm.1, bf16[3,8,128,128]{3,2,1,0:T(8,128)(2,1)} %op_hbm.1, s32[3,8]{1,0:T(4,128)} %col_hbm.1, s32[3,8]{1,0:T(4,128)} %mask_hbm.1, f32[384,128]{1,0:T(8,128)} %bitcast.7, s32[4,1,512]{2,1,0:T(1,128)} %bitcast.8, f32[4,1,512]{2,1,0:T(1,128)} %bitcast.9), custom_call_target="tpu_custom_call" | custom-call | tf_op jit(solution)/shard_map/pallas_call | solution.py:512
  69.1 0.6 copy.11
  69.7 0.6 copy.12

commit v6 on v5

--- a/solution.py
+++ b/solution.py
@@ -385,11 +385,13 @@
                 buf[i] = take(ring, sense, i) + mine
             hand(ring, sense, slot(h, k - 1), 1, buf.at[i])
 
-    def close(ring, mid):
+    def close(ring, mid, direct, own):
         for h in range(4):
             mine = ring[0][ring[2], h * 4 : h * 4 + 4].astype(F32)
             both = take(ring, 0, slot(h, 1)).astype(F32) + take(ring, 1, slot(h, 1)).astype(F32)
             mid[h * 4 : h * 4 + 4] = (mine + both).astype(BF)
+            for g in range(h * 4, h * 4 + 4):
+                pl.when(own != g)(direct((g - own + 16) % 16).start)
 
     def direct_z(o):
         g, device = group_xy(o)
@@ -424,10 +426,8 @@
     advance(rings[1], 3)
     advance(rings[0], 2)
     advance(rings[1], 2)
-    close(rings[0], z_mid)
-    send_direct(direct_z)
-    close(rings[1], y_mid)
-    send_direct(direct_y)
+    close(rings[0], z_mid, direct_z, gy)
+    close(rings[1], y_mid, direct_y, gz)
     z_in[gy] = z_mid[gy]
     y_in[gz] = y_mid[gz]
 

time: 70.4 us -> 70.2 us (level)
  no operation moved by 1% of the time
where the time goes in v6:
time: 70.2 us; the launch traced here: 70.1 us
  Pallas kernels  68.3 us (97%)
  local copies, waits for them, and re-layouts  1.2 us (2%)
    pallas_call x1, Pallas kernels, body(): pl.pallas_call(kernel, out_shape=(jax.ShapeDtypeStruct((16, 512), F32), j...  68.3 us

profile of v6, /device:TPU:8, one launch (start us, length us, event | category | flops | bytes accessed | tf_op | source)
XLA Modules:
  0.0 70.1 jit_solution(5541914303792905710)
XLA Ops:
  0.6 68.3 %shard_map.86 = (f32[16,512]{1,0:T(8,128)S(1)}, f32[4,128]{1,0:T(4,128)S(1)}) custom-call(bf16[384,512]{1,0:T(8,128)(2,1)} %e_hbm.1, bf16[3,8,128,128]{3,2,1,0:T(8,128)(2,1)} %op_hbm.1, s32[3,8]{1,0:T(4,128)} %col_hbm.1, s32[3,8]{1,0:T(4,128)} %mask_hbm.1, f32[384,128]{1,0:T(8,128)} %bitcast.7, s32[4,1,512]{2,1,0:T(1,128)} %bitcast.8, f32[4,1,512]{2,1,0:T(1,128)} %bitcast.9), custom_call_target="tpu_custom_call" | custom-call | tf_op jit(solution)/shard_map/pallas_call | solution.py:512
  68.9 0.6 copy.11
  69.6 0.6 copy.12
